TPU v7x, 32 devices: a whole 2x2x4 slice. The times are simulated.
32 devices in a mesh: sky: 2 (over x), seg: 16 (over z, y, core).
Axes of the slice: x: 2, y: 2, z: 4, core: 2. Of those that a mesh axis runs over, the one named last changes fastest.
Arguments:
- strain_series: bfloat16 [32, 2, 65536], P(('sky', 'seg')), parts along dimension 0, may hold values from -6 to 6
- antenna: float32 [32, 2, 65536], P(('sky', 'seg')), parts along dimension 0, may hold values from -160 to 160, as said below
- drift: int32 [32, 6], P(('sky', 'seg')), parts along dimension 0, may hold values from -2 to 2
- tracks: int32 [64, 16], replicated, may hold values from 0 to 5
Outputs:
- track_stat: float32 [128, 65536], P('sky', 'seg'), parts along dimension 0
There are 2 independent parts, one for each index of `sky`. A program takes and returns all parts, laid end to end along the dimension named above; an argument that names none is the same for every part. Nothing has to cross between parts.
Inputs may be any that keep to these rules, and one draw needn't show every extreme that they name: `antenna`: row 0 holds the a weights, row 1 the b weights of each segment.
All inputs are finite; a program needn't handle non-finite values.
Results may differ from a plain program's by a relative error of at most 0.0015.
Values sent between devices are 32-bit elements; how exact they have to be, the bound alone decides.
A program may use at most 192 MiB of HBM per device.

v0:
```python
import functools
import math

import jax
import jax.numpy as jnp
import numpy as np
from jax import lax
from jax.experimental import pallas as pl
from jax.experimental.pallas import tpu as pltpu
from jax.sharding import PartitionSpec as P

DFT_ROWS = 256
BLK = 128
DMAX = 2
KCOH = 6
PAD = 8

chirp_step = 3.0
tiny_eps = 1e-06


def dft_table(rows):
    index = np.arange(rows, dtype=np.int64)
    angle = np.float32(2.0 * math.pi / rows) * (index[:, None] * index[None, :] % rows).astype(np.float32)
    cos, sin = np.cos(angle), np.sin(angle)
    return np.block([[cos, sin], [-sin, cos]]).astype(jnp.bfloat16)


def twist_table(points, first_rows):
    second_rows = points // first_rows
    outer = np.arange(first_rows, dtype=np.int64)
    inner = np.arange(second_rows, dtype=np.int64)
    angle = np.float32(2.0 * math.pi / points) * (outer[:, None] * inner[None, :] % points).astype(np.float32)
    return np.stack([np.cos(angle), np.sin(angle)]).astype(np.float32)


def chirp_table(points, first_rows):
    position = np.arange(points, dtype=np.float32) / np.float32(points)
    rate = (np.arange(KCOH // 2, KCOH, dtype=np.float32) - np.float32((KCOH - 1) / 2.0)) * np.float32(chirp_step)
    phases = (np.float32(2.0 * math.pi) * rate)[:, None] * (position * position)[None, :]
    both = np.stack([np.cos(phases), np.sin(phases)], 1).astype(np.float32)
    return both.reshape(KCOH // 2, 2, first_rows, points // first_rows)


def kernel(
    count, drift_ref, series_ref, antenna_ref, chirp_ref, twist_ref, first_ref, second_ref, tracks_ref, out_ref,
    strain, weights, weighted, spread, middle, padded, send, recv, send_sem, recv_sem,
):
    _, first_rows, second_rows = strain.shape
    rows = second_rows // count
    points = first_rows * second_rows
    halves = first_rows // BLK
    sky = lax.axis_index("sky")
    me = lax.axis_index("seg")

    barrier = pltpu.get_barrier_semaphore()

    def greet(step, carry):
        pl.semaphore_signal(
            barrier, inc=1, device_id=(sky, lax.rem(me + step, count)), device_id_type=pl.DeviceIdType.MESH
        )
        return carry

    lax.fori_loop(1, count, greet, 0)

    pieces = second_rows // BLK
    for which in range(2):
        for piece in range(pieces):
            lanes = slice(piece * BLK, (piece + 1) * BLK)
            lines = pl.ds(piece, first_rows, stride=pieces)
            strain[which, :, lanes] = series_ref[lines, which, :]
            weights[which, :, lanes] = antenna_ref[lines, which, :]

    weight_a, weight_b = weights[0], weights[1]
    total = lambda value: jnp.sum(jnp.sum(value, axis=0, keepdims=True), axis=1, keepdims=True)
    aa = total(weight_a * weight_a) / points + tiny_eps
    bb = total(weight_b * weight_b) / points + tiny_eps
    ab = total(weight_a * weight_b) / points
    scale = 1.0 / (points * jnp.maximum(aa * bb - ab * ab, 0.1 * aa * bb))
    coef_a, coef_b, coef_ab = bb * scale, aa * scale, 2.0 * ab * scale

    for half in range(halves):
        padded[half, :PAD] = jnp.zeros((PAD, BLK), jnp.float32)
        padded[half, PAD + second_rows :] = jnp.zeros((PAD, BLK), jnp.float32)

    pl.semaphore_wait(barrier, count - 1)

    def one_rate(k, carry):
        upper = k >= KCOH // 2
        level = jnp.where(upper, k - KCOH // 2, KCOH // 2 - 1 - k)
        sign = jnp.where(upper, 1.0, -1.0)
        chirp_cos = chirp_ref[level, 0]
        chirp_sin = chirp_ref[level, 1] * sign
        real, imag = strain[0], strain[1]
        demod_real = real * chirp_cos + imag * chirp_sin
        demod_imag = imag * chirp_cos - real * chirp_sin
        for which in range(2):
            weight = weights[which]
            columns = slice(which * second_rows, (which + 1) * second_rows)
            weighted[:first_rows, columns] = (weight * demod_real).astype(jnp.bfloat16)
            weighted[first_rows:, columns] = (weight * demod_imag).astype(jnp.bfloat16)
        spread[...] = jnp.dot(first_ref[...], weighted[...], preferred_element_type=jnp.float32)
        twist_cos, twist_sin = twist_ref[0], twist_ref[1]
        for which in range(2):
            columns = slice(which * second_rows, (which + 1) * second_rows)
            one_real, one_imag = spread[:first_rows, columns], spread[first_rows:, columns]
            lines = slice(which * first_rows, (which + 1) * first_rows)
            middle[lines, :second_rows] = (one_real * twist_cos + one_imag * twist_sin).astype(jnp.bfloat16)
            middle[lines, second_rows:] = (one_imag * twist_cos - one_real * twist_sin).astype(jnp.bfloat16)
        spread[...] = lax.dot_general(
            second_ref[...], middle[...], (((1,), (1,)), ((), ())), preferred_element_type=jnp.float32
        )
        for half in range(halves):
            at_a = slice(half * BLK, (half + 1) * BLK)
            at_b = slice(first_rows + half * BLK, first_rows + (half + 1) * BLK)
            a_real, a_imag = spread[:second_rows, at_a], spread[second_rows:, at_a]
            b_real, b_imag = spread[:second_rows, at_b], spread[second_rows:, at_b]
            padded[half, PAD : PAD + second_rows] = (
                coef_a * (a_real * a_real + a_imag * a_imag)
                + coef_b * (b_real * b_real + b_imag * b_imag)
                - coef_ab * (a_real * b_real + a_imag * b_imag)
            )
        shift = drift_ref[0, k]

        def place(peer, inner):
            for half in range(halves):
                block = half - shift + halves * PAD
                source = lax.rem(block, halves)
                start = lax.div(block, halves) + rows * peer
                send[k, peer, :, half * BLK : (half + 1) * BLK] = padded[source, pl.ds(start, rows), :]
            return inner

        lax.fori_loop(0, count, place, 0)

        def ship(step, inner):
            peer = lax.rem(me + step, count)
            pltpu.make_async_remote_copy(
                src_ref=send.at[k, peer],
                dst_ref=recv.at[k, me],
                send_sem=send_sem.at[k],
                recv_sem=recv_sem.at[k],
                device_id=(sky, peer),
                device_id_type=pl.DeviceIdType.MESH,
            ).start()
            return inner

        lax.fori_loop(1, count, ship, 0)
        pltpu.make_async_copy(send.at[k, me], recv.at[k, me], recv_sem.at[k]).start()
        return carry

    lax.fori_loop(0, KCOH, one_rate, 0)

    out_ref[...] = jnp.zeros_like(out_ref)
    add_rows = lambda pick, value: lax.dot_general(
        pick, value, (((0,), (0,)), ((), ())), preferred_element_type=jnp.float32
    )

    def collect(k, carry):
        pltpu.make_async_copy(recv.at[k], recv.at[k], recv_sem.at[k]).wait()
        pick = jnp.where(tracks_ref[...] == k, 1.0, 0.0).astype(jnp.bfloat16)
        for row in range(rows):
            value = recv[k, :, row, :]
            high = value.astype(jnp.bfloat16)
            low = (value - high.astype(jnp.float32)).astype(jnp.bfloat16)
            columns = slice(row * first_rows, (row + 1) * first_rows)
            out_ref[:, columns] += add_rows(pick, high) + add_rows(pick, low)
        return carry

    lax.fori_loop(0, KCOH, collect, 0)

    for k in range(KCOH):
        part = send.at[k, pl.ds(0, count - 1)]
        pltpu.make_async_copy(part, part, send_sem.at[k]).wait()


def local(count, strain_series, antenna, drift, tracks):
    points = strain_series.shape[2]
    first_rows, second_rows = DFT_ROWS, points // DFT_ROWS
    segments = tracks.shape[1]
    rows = second_rows // count
    blocked = lambda array: array.reshape(2, points // BLK, BLK).transpose(1, 0, 2)
    vmem = pl.BlockSpec(memory_space=pltpu.VMEM)
    summed = pl.pallas_call(
        functools.partial(kernel, count),
        out_shape=pltpu.VMEM((tracks.shape[0], points // count), jnp.float32),
        in_specs=[pl.BlockSpec(memory_space=pltpu.SMEM)] + [vmem] * 7,
        out_specs=vmem,
        scratch_shapes=[
            pltpu.VMEM((2, first_rows, second_rows), jnp.float32),
            pltpu.VMEM((2, first_rows, second_rows), jnp.float32),
            pltpu.VMEM((2 * first_rows, 2 * second_rows), jnp.bfloat16),
            pltpu.VMEM((2 * max(first_rows, second_rows), 2 * max(first_rows, second_rows)), jnp.float32),
            pltpu.VMEM((2 * first_rows, 2 * second_rows), jnp.bfloat16),
            pltpu.VMEM((first_rows // BLK, second_rows + 2 * PAD, BLK), jnp.float32),
            pltpu.VMEM((KCOH, count, rows, first_rows), jnp.float32),
            pltpu.VMEM((KCOH, count, rows, first_rows), jnp.float32),
            pltpu.SemaphoreType.DMA((KCOH,)),
            pltpu.SemaphoreType.DMA((KCOH,)),
        ],
        compiler_params=pltpu.CompilerParams(
            collective_id=0, has_side_effects=True, vmem_limit_bytes=60 << 20
        ),
    )(
        drift,
        blocked(strain_series.astype(jnp.float32)),
        blocked(antenna),
        jnp.asarray(chirp_table(points, first_rows)),
        jnp.asarray(twist_table(points, first_rows)),
        jnp.asarray(dft_table(first_rows)),
        jnp.asarray(dft_table(second_rows)),
        tracks.T,
    )
    return summed / segments


def solution(mesh):
    return jax.shard_map(
        functools.partial(local, mesh.shape["seg"]),
        mesh=mesh,
        in_specs=(
            P(("sky", "seg"), None, None),
            P(("sky", "seg"), None, None),
            P(("sky", "seg"), None),
            P(),
        ),
        out_specs=P("sky", "seg"),
        check_vma=False,
    )
```

profile of v0, /device:TPU:11, one launch (start us, length us, event | category | flops | bytes accessed | tf_op | source)
XLA Modules:
  0.0 46.0 jit_solution(6155728938581517257)
XLA Ops:
  0.0 1.9 %convert_bitcast_fusion.series_ref = f32[512,2,128]{2,1,0:T(2,128)} fusion(bf16[1,2,65536]{2,1,0:T(2,128)(2,1)} %param.8), kind=kLoop, calls=%fused_computation | loop fusion | flops 131072 | bytes 786432 | tf_op jit(solution)/shard_map/transpose | solution.py:181
  1.9 43.0 %shard_map.82 = f32[64,4096]{1,0:T(8,128)S(1)} custom-call(s32[1,6]{1,0:T(1,128)} %drift_ref.1, f32[512,2,128]{2,1,0:T(2,128)} %convert_bitcast_fusion.series_ref, f32[512,2,128]{2,1,0:T(2,128)} %bitcast.9, f32[3,2,256,256]{3,2,1,0:T(8,128)} %constant.9.clone.chirp_ref, f32[2,256,256]{2,1,0:T(8,128)} %constant.10.clone.twist_ref, ...), custom_call_target="tpu_custom_call" | custom-call | tf_op jit(solution)/shard_map/pallas_call | solution.py:183
  44.9 1.1 %broadcast_multiply_fusion = f32[64,4096]{1,0:T(8,128)} fusion(f32[64,4096]{1,0:T(8,128)S(1)} %shard_map.82), kind=kLoop, calls=%fused_computation.1 | loop fusion | flops 262144 | bytes 2097152 | tf_op jit(solution)/shard_map/div | solution.py:213
where the time goes:
time: 46.9 us; the launch traced here: 46 us
  Pallas kernels  43 us (92%)
  other arithmetic  2.98 us (6%)
    pallas_call x1, Pallas kernels, local(): pl.pallas_call(functools.partial(kernel, count), out_shape=pltpu.VMEM((tr...  43 us
    transpose x1, other arithmetic, local(): array.reshape(2, points // BLK, BLK).transpose(1, 0, 2)  1.92 us
    div x1, other arithmetic, local(): return summed / segments  1.06 us

commit v1 on v0

v1 whole, which is shorter than its diff:
```python
import functools
import math

import jax
import jax.numpy as jnp
import numpy as np
from jax import lax
from jax.experimental import pallas as pl
from jax.experimental.pallas import tpu as pltpu
from jax.sharding import PartitionSpec as P

DFT_ROWS = 256
BLK = 128
KCOH = 6
LEVELS = KCOH // 2
PAD = 8
HALO = 16
MESH = pl.DeviceIdType.MESH

chirp_step = 3.0
tiny_eps = 1e-06


def dft_table(rows):
    index = np.arange(rows, dtype=np.int64)
    angle = np.float32(2.0 * math.pi / rows) * (index[:, None] * index[None, :] % rows).astype(np.float32)
    cos, sin = np.cos(angle), np.sin(angle)
    return np.block([[cos, sin], [-sin, cos]]).astype(jnp.bfloat16)


def twist_table(points, first_rows):
    second_rows = points // first_rows
    outer = np.arange(first_rows, dtype=np.int64)
    inner = np.arange(second_rows, dtype=np.int64)
    angle = np.float32(2.0 * math.pi / points) * (outer[:, None] * inner[None, :] % points).astype(np.float32)
    return np.stack([np.cos(angle), np.sin(angle)]).astype(np.float32)


def chirp_table(points, first_rows):
    position = np.arange(points, dtype=np.float32) / np.float32(points)
    rate = (np.arange(LEVELS, KCOH, dtype=np.float32) - np.float32((KCOH - 1) / 2.0)) * np.float32(chirp_step)
    phases = (np.float32(2.0 * math.pi) * rate)[:, None] * (position * position)[None, :]
    both = np.stack([np.cos(phases), np.sin(phases)], 1).astype(np.float32)
    return both.reshape(LEVELS, 2, first_rows, points // first_rows)


def kernel(
    count, drift_hbm, series_hbm, antenna_hbm, chirp_hbm, twist_hbm, table_hbm, tracks_hbm, out_ref,
    drift, series_in, series, antenna, chirp, twist, table, tracks,
    strain, weights, weighted, spread, middle, spectra, padded,
    send, recv, gather, total_far, from_far,
    load_sem, chirp_sem, send_sem, far_sem, near_sem, gather_sem, total_sem,
):
    _, first_rows, second_rows = strain.shape
    rows = second_rows // count
    half_count = count // 2
    half_rows = second_rows // 2
    points = first_rows * second_rows
    halves = first_rows // BLK
    sky = lax.axis_index("sky")
    me = lax.axis_index("seg")
    side = lax.div(me, half_count)
    place_in = lax.rem(me, half_count)
    far = (1 - side) * half_count
    near = side * half_count
    mirror = far + place_in

    loads = [
        pltpu.make_async_copy(source, target, load_sem.at[index])
        for index, (source, target) in enumerate([
            (series_hbm, series_in), (antenna_hbm, antenna), (table_hbm, table), (twist_hbm, twist), (drift_hbm, drift),
            (tracks_hbm, tracks),
        ])
    ]
    chirp_load = lambda level: pltpu.make_async_copy(chirp_hbm.at[level], chirp.at[level], chirp_sem.at[level])
    loads[0].start()
    loads[1].start()
    chirp_load(0).start()
    for load in loads[2:]:
        load.start()

    barrier = pltpu.get_barrier_semaphore()

    def greet(step, carry):
        pl.semaphore_signal(barrier, inc=1, device_id=(sky, lax.rem(me + step, count)), device_id_type=MESH)
        return carry

    lax.fori_loop(1, count, greet, 0)

    for which in range(2):
        for half in range(halves):
            padded[which, half, :PAD] = jnp.zeros((PAD, BLK), jnp.float32)
            padded[which, half, PAD + second_rows :] = jnp.zeros((PAD, BLK), jnp.float32)
    send[1] = jnp.zeros(send.shape[1:], jnp.float32)

    loads[0].wait()
    series[...] = series_in[...].astype(jnp.float32)
    loads[1].wait()
    pieces = second_rows // BLK
    for which in range(2):
        for piece in range(pieces):
            lanes = slice(piece * BLK, (piece + 1) * BLK)
            lines = pl.ds(piece, first_rows, stride=pieces)
            strain[which, :, lanes] = series[lines, which, :]
            weights[which, :, lanes] = antenna[lines, which, :]

    weight_a, weight_b = weights[0], weights[1]
    total = lambda value: jnp.sum(jnp.sum(value, axis=0, keepdims=True), axis=1, keepdims=True)
    aa = total(weight_a * weight_a) / points + tiny_eps
    bb = total(weight_b * weight_b) / points + tiny_eps
    ab = total(weight_a * weight_b) / points
    scale = 1.0 / (points * jnp.maximum(aa * bb - ab * ab, 0.1 * aa * bb))
    coef_a, coef_b, coef_ab = bb * scale, aa * scale, 2.0 * ab * scale

    for load in loads[2:]:
        load.wait()
    for level in range(1, LEVELS):
        chirp_load(level).start()

    def second_stage(start, size):
        start = pl.multiple_of(start, HALO)
        for which in range(4):
            for part in range(2):
                spectra[which, part, :size] = lax.dot_general(
                    table[pl.ds(part * second_rows + start, size), :], middle[which], (((1,), (1,)), ((), ())),
                    preferred_element_type=jnp.float32,
                )
        for which in range(2):
            a_real, a_imag = spectra[2 * which, 0, :size], spectra[2 * which, 1, :size]
            b_real, b_imag = spectra[2 * which + 1, 0, :size], spectra[2 * which + 1, 1, :size]
            value = (
                coef_a * (a_real * a_real + a_imag * a_imag)
                + coef_b * (b_real * b_real + b_imag * b_imag)
                - coef_ab * (a_real * b_real + a_imag * b_imag)
            )
            for half in range(halves):
                padded[which, half, pl.ds(PAD + start, size), :] = value[:, half * BLK : (half + 1) * BLK]

    def place(level, first_device):
        for which in (1, 0):
            shift = drift[0, (LEVELS + level) if which == 0 else (LEVELS - 1 - level)]
            channel = 2 * level + which
            for half in range(halves):
                block = half - shift + halves * PAD
                source = lax.rem(block, halves)
                start = lax.div(block, halves)
                lanes = slice(half * BLK, (half + 1) * BLK)
                if rows % 8 == 0:
                    devices = pl.ds(first_device, half_count)
                    value = padded[which, source, pl.ds(start + first_device * rows, half_rows), :]
                    base = send[1, devices, :, lanes]
                    send[channel, devices, :, lanes] = value.reshape(half_count, rows, BLK) - base
                else:
                    def one(step, carry, which=which, channel=channel, source=source, start=start, lanes=lanes):
                        peer = first_device + step
                        value = padded[which, source, pl.ds(start + peer * rows, rows), :]
                        send[channel, peer, :, lanes] = value - send[1, peer, :, lanes]
                        return carry

                    lax.fori_loop(0, half_count, one, 0)

    def push(source, target, done, arrived, peer):
        pltpu.make_async_remote_copy(
            src_ref=source, dst_ref=target, send_sem=done, recv_sem=arrived, device_id=(sky, peer), device_id_type=MESH
        ).start()

    def ship_far(channel):
        def one(step, carry):
            peer = far + lax.rem(place_in + step, half_count)
            push(send.at[channel, peer], recv.at[channel, me], send_sem.at[channel], far_sem.at[channel], peer)
            return carry

        lax.fori_loop(0, half_count, one, 0)

    def ship_near(channel):
        def one(step, carry):
            peer = near + lax.rem(place_in + step, half_count)
            push(send.at[channel, peer], recv.at[channel, me], send_sem.at[channel], near_sem.at[channel], peer)
            return carry

        lax.fori_loop(1, half_count, one, 0)
        pltpu.make_async_copy(send.at[channel, me], recv.at[channel, me], near_sem.at[channel]).start()

    def ship_base():
        def one(step, carry):
            other = lax.rem(place_in + step, half_count)
            push(send.at[1, far + other], gather.at[place_in], send_sem.at[1], gather_sem, near + other)
            return carry

        lax.fori_loop(1, half_count, one, 0)
        pltpu.make_async_copy(send.at[1, mirror], gather.at[place_in], gather_sem).start()

    def one_level(level, carry):
        chirp_load(level).wait()
        chirp_cos, chirp_sin = chirp[level, 0], chirp[level, 1]
        real, imag = strain[0], strain[1]
        real_cos, imag_sin = real * chirp_cos, imag * chirp_sin
        imag_cos, real_sin = imag * chirp_cos, real * chirp_sin
        demods = ((real_cos + imag_sin, imag_cos - real_sin), (real_cos - imag_sin, imag_cos + real_sin))
        for which in range(4):
            weight = weights[which % 2]
            for part in range(2):
                lines = slice(part * first_rows, (part + 1) * first_rows)
                weighted[which, lines, :] = (weight * demods[which // 2][part]).astype(jnp.bfloat16)
        twist_cos, twist_sin = twist[0], twist[1]
        for which in range(4):
            spread[which] = jnp.dot(table[...], weighted[which], preferred_element_type=jnp.float32)
            one_real, one_imag = spread[which, :first_rows], spread[which, first_rows:]
            middle[which, :, :second_rows] = (one_real * twist_cos + one_imag * twist_sin).astype(jnp.bfloat16)
            middle[which, :, second_rows:] = (one_imag * twist_cos - one_real * twist_sin).astype(jnp.bfloat16)

        second_stage((1 - side) * (half_rows - HALO), half_rows + HALO)
        place(level, far)

        @pl.when(level == 0)
        def _():
            pl.semaphore_wait(barrier, count - 1)

        ship_far(2 * level)

        @pl.when(level > 0)
        def _():
            ship_far(2 * level + 1)

        second_stage(side * (half_rows + HALO), half_rows - HALO)
        place(level, near)

        @pl.when(level == 0)
        def _():
            ship_base()

        ship_near(2 * level + 1)
        ship_near(2 * level)

        @pl.when(level == LEVELS - 2)
        def _():
            pltpu.make_async_copy(gather, gather, gather_sem).wait()
            total_far[...] = jnp.sum(gather[...], axis=0)
            push(total_far, from_far, total_sem.at[0], total_sem.at[1], mirror)

        return carry

    lax.fori_loop(0, LEVELS, one_level, 0)

    out_ref[...] = jnp.zeros_like(out_ref)
    far_devices, near_devices = pl.ds(far, half_count), pl.ds(near, half_count)
    await_bytes = lambda part, arrived: pltpu.make_async_copy(part, part, arrived).wait()

    def collect(step, carry):
        channel = jnp.where(step == 0, 0, step + 1)

        @pl.when(step == KCOH - 2)
        def _():
            await_bytes(recv.at[1, near_devices], near_sem.at[1])
            await_bytes(from_far, total_sem.at[1])
            base = jnp.sum(recv[1, near_devices], axis=0) + from_far[...]
            for row in range(rows):
                columns = slice(row * first_rows, (row + 1) * first_rows)
                out_ref[:, columns] += base[row : row + 1, :]

        await_bytes(recv.at[channel, near_devices], near_sem.at[channel])
        await_bytes(recv.at[channel, far_devices], far_sem.at[channel])
        level = lax.div(channel, 2)
        rate = jnp.where(lax.rem(channel, 2) == 0, LEVELS + level, LEVELS - 1 - level)
        pick = jnp.where(tracks[...] == rate, 1.0, 0.0).astype(jnp.bfloat16)
        pick = jnp.concatenate([pick, pick], axis=0)
        for row in range(rows):
            value = recv[channel, :, row, :]
            high = value.astype(jnp.bfloat16)
            low = (value - high.astype(jnp.float32)).astype(jnp.bfloat16)
            columns = slice(row * first_rows, (row + 1) * first_rows)
            out_ref[:, columns] += lax.dot_general(
                pick, jnp.concatenate([high, low], axis=0), (((0,), (0,)), ((), ())), preferred_element_type=jnp.float32
            )
        return carry

    lax.fori_loop(0, KCOH - 1, collect, 0)

    for channel in range(KCOH):
        if channel == 1:
            part = send.at[1, pl.ds(0, 2 * (half_count - 1))]
        else:
            part = send.at[channel, pl.ds(0, count - 1)]
        await_bytes(part, send_sem.at[channel])
    await_bytes(total_far, total_sem.at[0])


def local(count, strain_series, antenna, drift, tracks):
    points = strain_series.shape[2]
    first_rows, second_rows = DFT_ROWS, points // DFT_ROWS
    segments = tracks.shape[1]
    rows = second_rows // count
    blocked = lambda array: array.reshape(2, points // BLK, BLK).transpose(1, 0, 2)
    hbm = pl.BlockSpec(memory_space=pl.ANY)
    chirps = chirp_table(points, first_rows)
    block = (points // BLK, 2, BLK)
    summed = pl.pallas_call(
        functools.partial(kernel, count),
        out_shape=pltpu.VMEM((tracks.shape[0], points // count), jnp.float32),
        in_specs=[hbm] * 7,
        out_specs=pl.BlockSpec(memory_space=pltpu.VMEM),
        scratch_shapes=[
            pltpu.SMEM(drift.shape, jnp.int32),
            pltpu.VMEM(block, jnp.bfloat16),
            pltpu.VMEM(block, jnp.float32),
            pltpu.VMEM(block, jnp.float32),
            pltpu.VMEM(chirps.shape, jnp.float32),
            pltpu.VMEM((2, first_rows, second_rows), jnp.float32),
            pltpu.VMEM((2 * first_rows, 2 * first_rows), jnp.bfloat16),
            pltpu.VMEM((segments, tracks.shape[0]), jnp.int32),
            pltpu.VMEM((2, first_rows, second_rows), jnp.float32),
            pltpu.VMEM((2, first_rows, second_rows), jnp.float32),
            pltpu.VMEM((4, 2 * first_rows, second_rows), jnp.bfloat16),
            pltpu.VMEM((4, 2 * first_rows, second_rows), jnp.float32),
            pltpu.VMEM((4, first_rows, 2 * second_rows), jnp.bfloat16),
            pltpu.VMEM((4, 2, second_rows // 2 + HALO, first_rows), jnp.float32),
            pltpu.VMEM((2, first_rows // BLK, second_rows + 2 * PAD, BLK), jnp.float32),
            pltpu.VMEM((KCOH, count, rows, first_rows), jnp.float32),
            pltpu.VMEM((KCOH, count, rows, first_rows), jnp.float32),
            pltpu.VMEM((count // 2, rows, first_rows), jnp.float32),
            pltpu.VMEM((rows, first_rows), jnp.float32),
            pltpu.VMEM((rows, first_rows), jnp.float32),
            pltpu.SemaphoreType.DMA((6,)),
            pltpu.SemaphoreType.DMA((LEVELS,)),
            pltpu.SemaphoreType.DMA((KCOH,)),
            pltpu.SemaphoreType.DMA((KCOH,)),
            pltpu.SemaphoreType.DMA((KCOH,)),
            pltpu.SemaphoreType.DMA,
            pltpu.SemaphoreType.DMA((2,)),
        ],
        compiler_params=pltpu.CompilerParams(
            collective_id=0, has_side_effects=True, vmem_limit_bytes=60 << 20
        ),
    )(
        drift,
        blocked(strain_series),
        blocked(antenna),
        jnp.asarray(chirps),
        jnp.asarray(twist_table(points, first_rows)),
        jnp.asarray(dft_table(first_rows)),
        tracks.T,
    )
    return summed / segments


def solution(mesh):
    return jax.shard_map(
        functools.partial(local, mesh.shape["seg"]),
        mesh=mesh,
        in_specs=(
            P(("sky", "seg"), None, None),
            P(("sky", "seg"), None, None),
            P(("sky", "seg"), None),
            P(),
        ),
        out_specs=P("sky", "seg"),
        check_vma=False,
    )
```

time: 46.9 us -> 40.2 us (0.86)
  the two profiles are of different devices: /device:TPU:11 before, /device:TPU:0 now
where the time goes in v1:
time: 40.2 us; the launch traced here: 40 us
  Pallas kernels  39 us (97%)
  other arithmetic  1.06 us (3%)
    pallas_call x1, Pallas kernels, local(): pl.pallas_call(functools.partial(kernel, count), out_shape=pltpu.VMEM((tr...  39 us
    div x1, other arithmetic, local(): return summed / segments  1.06 us

profile of v1, /device:TPU:0, one launch (start us, length us, event | category | flops | bytes accessed | tf_op | source)
XLA Modules:
  0.0 40.0 jit_solution(10297860524797812761)
XLA Ops:
  0.0 39.0 %shard_map.73 = f32[64,4096]{1,0:T(8,128)S(1)} custom-call(s32[1,6]{1,0:T(1,128)} %drift_hbm.1, bf16[512,2,128]{2,1,0:T(2,128)(2,1)} %bitcast.8, f32[512,2,128]{2,1,0:T(2,128)} %bitcast.7, f32[3,2,256,256]{3,2,1,0:T(8,128)} %constant.9.clone.chirp_hbm, f32[2,256,256]{2,1,0:T(8,128)} %constant.10.clone.twist_hbm, bf16[512,512]{1,0:T(8,128)(2,1)} %constant.11.clone.table_hbm, ...), custom_call_target="tpu_custom_call" | custom-call | tf_op jit(solution)/shard_map/pallas_call | solution.py:297
  39.0 1.1 %broadcast_multiply_fusion = f32[64,4096]{1,0:T(8,128)} fusion(f32[64,4096]{1,0:T(8,128)S(1)} %shard_map.73), kind=kLoop, calls=%fused_computation | loop fusion | flops 262144 | bytes 2097152 | tf_op jit(solution)/shard_map/div | solution.py:343

commit v2 on v1

--- a/solution.py
+++ b/solution.py
@@ -166,7 +166,7 @@
 
     def ship_far(channel):
         def one(step, carry):
-            peer = far + lax.rem(place_in + step, half_count)
+            peer = jnp.where(side == 0, count - 1 - step, step)
             push(send.at[channel, peer], recv.at[channel, me], send_sem.at[channel], far_sem.at[channel], peer)
             return carry
 

time: 40.2 us -> 38.7 us (0.963)
  Pallas kernels: 39 us -> 37.5 us
    pallas_call x1, Pallas kernels: 39 us -> 37.5 us  [local(): pl.pallas_call(functools.partial(kernel, count), out_shape=pltpu.VMEM((tr...]
where the time goes in v2:
time: 38.7 us; the launch traced here: 38.6 us
  Pallas kernels  37.5 us (97%)
  other arithmetic  1.06 us (3%)
    pallas_call x1, Pallas kernels, local(): pl.pallas_call(functools.partial(kernel, count), out_shape=pltpu.VMEM((tr...  37.5 us
    div x1, other arithmetic, local(): return summed / segments  1.06 us

profile of v2, /device:TPU:0, one launch (start us, length us, event | category | flops | bytes accessed | tf_op | source)
XLA Modules:
  0.0 38.6 jit_solution(17943448867471198273)
XLA Ops:
  0.0 37.5 %shard_map.73 = f32[64,4096]{1,0:T(8,128)S(1)} custom-call(s32[1,6]{1,0:T(1,128)} %drift_hbm.1, bf16[512,2,128]{2,1,0:T(2,128)(2,1)} %bitcast.8, f32[512,2,128]{2,1,0:T(2,128)} %bitcast.7, f32[3,2,256,256]{3,2,1,0:T(8,128)} %constant.9.clone.chirp_hbm, f32[2,256,256]{2,1,0:T(8,128)} %constant.10.clone.twist_hbm, bf16[512,512]{1,0:T(8,128)(2,1)} %constant.11.clone.table_hbm, ...), custom_call_target="tpu_custom_call" | custom-call | tf_op jit(solution)/shard_map/pallas_call | solution.py:297
  37.5 1.1 %broadcast_multiply_fusion = f32[64,4096]{1,0:T(8,128)} fusion(f32[64,4096]{1,0:T(8,128)S(1)} %shard_map.73), kind=kLoop, calls=%fused_computation | loop fusion | flops 262144 | bytes 2097152 | tf_op jit(solution)/shard_map/div | solution.py:343

commit v3 on v2

--- a/solution.py
+++ b/solution.py
@@ -48,15 +48,15 @@
     count, drift_hbm, series_hbm, antenna_hbm, chirp_hbm, twist_hbm, table_hbm, tracks_hbm, out_ref,
     drift, series_in, series, antenna, chirp, twist, table, tracks,
     strain, weights, weighted, spread, middle, spectra, padded,
-    send, recv, gather, total_far, from_far,
+    send, recv, gather, total_far, from_far, picks, staged,
     load_sem, chirp_sem, send_sem, far_sem, near_sem, gather_sem, total_sem,
 ):
     _, first_rows, second_rows = strain.shape
-    rows = second_rows // count
+    halves = first_rows // BLK
+    blocks = second_rows * halves // count
     half_count = count // 2
     half_rows = second_rows // 2
     points = first_rows * second_rows
-    halves = first_rows // BLK
     sky = lax.axis_index("sky")
     me = lax.axis_index("seg")
     side = lax.div(me, half_count)
@@ -88,9 +88,8 @@
     lax.fori_loop(1, count, greet, 0)
 
     for which in range(2):
-        for half in range(halves):
-            padded[which, half, :PAD] = jnp.zeros((PAD, BLK), jnp.float32)
-            padded[which, half, PAD + second_rows :] = jnp.zeros((PAD, BLK), jnp.float32)
+        padded[which, :PAD] = jnp.zeros((PAD, BLK), jnp.float32)
+        padded[which, PAD + second_rows * halves :] = jnp.zeros((PAD, BLK), jnp.float32)
     send[1] = jnp.zeros(send.shape[1:], jnp.float32)
 
     loads[0].wait()
@@ -100,9 +99,9 @@
     for which in range(2):
         for piece in range(pieces):
             lanes = slice(piece * BLK, (piece + 1) * BLK)
-            lines = pl.ds(piece, first_rows, stride=pieces)
-            strain[which, :, lanes] = series[lines, which, :]
-            weights[which, :, lanes] = antenna[lines, which, :]
+            lines = pl.ds(2 * piece + which, first_rows, stride=2 * pieces)
+            strain[which, :, lanes] = series[lines, :]
+            weights[which, :, lanes] = antenna[lines, :]
 
     weight_a, weight_b = weights[0], weights[1]
     total = lambda value: jnp.sum(jnp.sum(value, axis=0, keepdims=True), axis=1, keepdims=True)
@@ -134,30 +133,25 @@
                 - coef_ab * (a_real * b_real + a_imag * b_imag)
             )
             for half in range(halves):
-                padded[which, half, pl.ds(PAD + start, size), :] = value[:, half * BLK : (half + 1) * BLK]
+                lines = pl.ds(PAD + halves * start + half, size, stride=halves)
+                padded[which, lines, :] = value[:, half * BLK : (half + 1) * BLK]
 
     def place(level, first_device):
         for which in (1, 0):
             shift = drift[0, (LEVELS + level) if which == 0 else (LEVELS - 1 - level)]
             channel = 2 * level + which
-            for half in range(halves):
-                block = half - shift + halves * PAD
-                source = lax.rem(block, halves)
-                start = lax.div(block, halves)
-                lanes = slice(half * BLK, (half + 1) * BLK)
-                if rows % 8 == 0:
-                    devices = pl.ds(first_device, half_count)
-                    value = padded[which, source, pl.ds(start + first_device * rows, half_rows), :]
-                    base = send[1, devices, :, lanes]
-                    send[channel, devices, :, lanes] = value.reshape(half_count, rows, BLK) - base
-                else:
-                    def one(step, carry, which=which, channel=channel, source=source, start=start, lanes=lanes):
-                        peer = first_device + step
-                        value = padded[which, source, pl.ds(start + peer * rows, rows), :]
-                        send[channel, peer, :, lanes] = value - send[1, peer, :, lanes]
-                        return carry
-
-                    lax.fori_loop(0, half_count, one, 0)
+            if blocks % 8 == 0:
+                devices = pl.ds(first_device, half_count)
+                value = padded[which, pl.ds(PAD + first_device * blocks - shift, half_count * blocks), :]
+                send[channel, devices] = value.reshape(half_count, blocks, BLK) - send[1, devices]
+            else:
+                def one(step, carry, which=which, channel=channel, shift=shift):
+                    peer = first_device + step
+                    value = padded[which, pl.ds(PAD + peer * blocks - shift, blocks), :]
+                    send[channel, peer] = value - send[1, peer]
+                    return carry
+
+                lax.fori_loop(0, half_count, one, 0)
 
     def push(source, target, done, arrived, peer):
         pltpu.make_async_remote_copy(
@@ -242,39 +236,57 @@
 
     lax.fori_loop(0, LEVELS, one_level, 0)
 
-    out_ref[...] = jnp.zeros_like(out_ref)
     far_devices, near_devices = pl.ds(far, half_count), pl.ds(near, half_count)
     await_bytes = lambda part, arrived: pltpu.make_async_copy(part, part, arrived).wait()
 
-    def collect(step, carry):
-        channel = jnp.where(step == 0, 0, step + 1)
-
-        @pl.when(step == KCOH - 2)
-        def _():
-            await_bytes(recv.at[1, near_devices], near_sem.at[1])
-            await_bytes(from_far, total_sem.at[1])
-            base = jnp.sum(recv[1, near_devices], axis=0) + from_far[...]
-            for row in range(rows):
-                columns = slice(row * first_rows, (row + 1) * first_rows)
-                out_ref[:, columns] += base[row : row + 1, :]
-
+    channels = [channel for channel in range(KCOH) if channel != 1]
+    chosen = []
+    for channel in channels:
+        rate = LEVELS + channel // 2 if channel % 2 == 0 else LEVELS - 1 - channel // 2
+        chosen += [jnp.where(tracks[...] == rate, 1.0, 0.0).astype(jnp.bfloat16)] * 2
+    chosen = jnp.concatenate(chosen, axis=0)
+    names = tracks.shape[1]
+    same = lax.broadcasted_iota(jnp.int32, (names, names), 0) == lax.broadcasted_iota(jnp.int32, (names, names), 1)
+    picks[...] = lax.dot_general(
+        jnp.where(same, 1.0, 0.0).astype(jnp.bfloat16), chosen, (((1,), (1,)), ((), ())), preferred_element_type=jnp.float32
+    ).astype(jnp.bfloat16)
+
+    def stage(step, channel):
         await_bytes(recv.at[channel, near_devices], near_sem.at[channel])
         await_bytes(recv.at[channel, far_devices], far_sem.at[channel])
-        level = lax.div(channel, 2)
-        rate = jnp.where(lax.rem(channel, 2) == 0, LEVELS + level, LEVELS - 1 - level)
-        pick = jnp.where(tracks[...] == rate, 1.0, 0.0).astype(jnp.bfloat16)
-        pick = jnp.concatenate([pick, pick], axis=0)
-        for row in range(rows):
-            value = recv[channel, :, row, :]
+        line = step * 2 * count if isinstance(step, int) else pl.multiple_of(step * 2 * count, 2 * count)
+        arrived = recv.at[channel].reshape(count * blocks, BLK) if blocks % 8 == 0 else None
+        for block in range(blocks):
+            if blocks % 8 == 0:
+                value = arrived[pl.ds(block, count, stride=blocks), :]
+            else:
+                value = recv[channel, :, block, :]
             high = value.astype(jnp.bfloat16)
-            low = (value - high.astype(jnp.float32)).astype(jnp.bfloat16)
-            columns = slice(row * first_rows, (row + 1) * first_rows)
-            out_ref[:, columns] += lax.dot_general(
-                pick, jnp.concatenate([high, low], axis=0), (((0,), (0,)), ((), ())), preferred_element_type=jnp.float32
-            )
+            lanes = slice(block * BLK, (block + 1) * BLK)
+            staged[pl.ds(line, count), lanes] = high
+            staged[pl.ds(line + count, count), lanes] = (value - high.astype(jnp.float32)).astype(jnp.bfloat16)
+
+    def stage_one(step, carry):
+        stage(step, jnp.where(step == 0, 0, step + 1))
         return carry
 
-    lax.fori_loop(0, KCOH - 1, collect, 0)
+    lax.fori_loop(0, KCOH - 2, stage_one, 0)
+    await_bytes(recv.at[1, near_devices], near_sem.at[1])
+    await_bytes(from_far, total_sem.at[1])
+    base = jnp.sum(recv[1, near_devices], axis=0) + from_far[...]
+    early = (KCOH - 2) * 2 * count
+    width = halves * BLK
+    parts = blocks // halves
+    for part in range(parts):
+        columns = slice(part * width, (part + 1) * width)
+        line = jnp.concatenate([base[part * halves + half : part * halves + half + 1, :] for half in range(halves)], axis=1)
+        out_ref[:, columns] = line + jnp.dot(
+            picks[:, :early], staged[:early, columns], preferred_element_type=jnp.float32
+        )
+    stage(KCOH - 2, channels[-1])
+    for part in range(parts):
+        columns = slice(part * width, (part + 1) * width)
+        out_ref[:, columns] += jnp.dot(picks[:, early:], staged[early:, columns], preferred_element_type=jnp.float32)
 
     for channel in range(KCOH):
         if channel == 1:
@@ -289,11 +301,11 @@
     points = strain_series.shape[2]
     first_rows, second_rows = DFT_ROWS, points // DFT_ROWS
     segments = tracks.shape[1]
-    rows = second_rows // count
-    blocked = lambda array: array.reshape(2, points // BLK, BLK).transpose(1, 0, 2)
+    blocks = points // count // BLK
+    blocked = lambda array: array.reshape(2, points // BLK, BLK).transpose(1, 0, 2).reshape(2 * points // BLK, BLK)
     hbm = pl.BlockSpec(memory_space=pl.ANY)
     chirps = chirp_table(points, first_rows)
-    block = (points // BLK, 2, BLK)
+    block = (2 * points // BLK, BLK)
     summed = pl.pallas_call(
         functools.partial(kernel, count),
         out_shape=pltpu.VMEM((tracks.shape[0], points // count), jnp.float32),
@@ -314,12 +326,14 @@
             pltpu.VMEM((4, 2 * first_rows, second_rows), jnp.float32),
             pltpu.VMEM((4, first_rows, 2 * second_rows), jnp.bfloat16),
             pltpu.VMEM((4, 2, second_rows // 2 + HALO, first_rows), jnp.float32),
-            pltpu.VMEM((2, first_rows // BLK, second_rows + 2 * PAD, BLK), jnp.float32),
-            pltpu.VMEM((KCOH, count, rows, first_rows), jnp.float32),
-            pltpu.VMEM((KCOH, count, rows, first_rows), jnp.float32),
-            pltpu.VMEM((count // 2, rows, first_rows), jnp.float32),
-            pltpu.VMEM((rows, first_rows), jnp.float32),
-            pltpu.VMEM((rows, first_rows), jnp.float32),
+            pltpu.VMEM((2, points // BLK + 2 * PAD, BLK), jnp.float32),
+            pltpu.VMEM((KCOH, count, blocks, BLK), jnp.float32),
+            pltpu.VMEM((KCOH, count, blocks, BLK), jnp.float32),
+            pltpu.VMEM((count // 2, blocks, BLK), jnp.float32),
+            pltpu.VMEM((blocks, BLK), jnp.float32),
+            pltpu.VMEM((blocks, BLK), jnp.float32),
+            pltpu.VMEM((tracks.shape[0], (KCOH - 1) * 2 * count), jnp.bfloat16),
+            pltpu.VMEM(((KCOH - 1) * 2 * count, points // count), jnp.bfloat16),
             pltpu.SemaphoreType.DMA((6,)),
             pltpu.SemaphoreType.DMA((LEVELS,)),
             pltpu.SemaphoreType.DMA((KCOH,)),

time: 38.7 us -> 38 us (0.982)
  Pallas kernels: 37.5 us -> 36.7 us
    pallas_call x1, Pallas kernels: 37.5 us -> 36.7 us  [local(): pl.pallas_call(functools.partial(kernel, count), out_shape=pltpu.VMEM((tr...]
where the time goes in v3:
time: 38 us; the launch traced here: 37.8 us
  Pallas kernels  36.7 us (97%)
  other arithmetic  1.06 us (3%)
    pallas_call x1, Pallas kernels, local(): pl.pallas_call(functools.partial(kernel, count), out_shape=pltpu.VMEM((tr...  36.7 us
    div x1, other arithmetic, local(): return summed / segments  1.06 us

profile of v3, /device:TPU:0, one launch (start us, length us, event | category | flops | bytes accessed | tf_op | source)
XLA Modules:
  0.0 37.8 jit_solution(16455229750447664466)
XLA Ops:
  0.0 36.7 %shard_map.73 = f32[64,4096]{1,0:T(8,128)S(1)} custom-call(s32[1,6]{1,0:T(1,128)} %drift_hbm.1, bf16[1024,128]{1,0:T(8,128)(2,1)} %bitcast.12, f32[1024,128]{1,0:T(8,128)} %bitcast.11, f32[3,2,256,256]{3,2,1,0:T(8,128)} %constant.9.clone.chirp_hbm, f32[2,256,256]{2,1,0:T(8,128)} %constant.10.clone.twist_hbm, bf16[512,512]{1,0:T(8,128)(2,1)} %constant.11.clone.table_hbm, ...), custom_call_target="tpu_custom_call" | custom-call | tf_op jit(solution)/shard_map/pallas_call | solution.py:309
  36.7 1.1 %broadcast_multiply_fusion = f32[64,4096]{1,0:T(8,128)} fusion(f32[64,4096]{1,0:T(8,128)S(1)} %shard_map.73), kind=kLoop, calls=%fused_computation | loop fusion | flops 262144 | bytes 2097152 | tf_op jit(solution)/shard_map/div | solution.py:357

commit v4 on v3

--- a/solution.py
+++ b/solution.py
@@ -49,12 +49,17 @@
     drift, series_in, series, antenna, chirp, twist, table, tracks,
     strain, weights, weighted, spread, middle, spectra, padded,
     send, recv, gather, total_far, from_far, picks, staged,
-    load_sem, chirp_sem, send_sem, far_sem, near_sem, gather_sem, total_sem,
+    load_sem, chirp_sem, send_sem, far_sem, near_sem, gather_sem, total_sem, late_sem,
 ):
     _, first_rows, second_rows = strain.shape
     halves = first_rows // BLK
     blocks = second_rows * halves // count
     half_count = count // 2
+    early_count = half_count + half_count // 2
+    late_count = count - early_count
+    flat = blocks % 8 == 0
+    slot = lambda device: pl.ds(pl.multiple_of(device * blocks, blocks), blocks) if flat else device
+    span = lambda device: pl.ds(pl.multiple_of(device * blocks, blocks), half_count * blocks) if flat else pl.ds(device, half_count)
     half_rows = second_rows // 2
     points = first_rows * second_rows
     sky = lax.axis_index("sky")
@@ -81,16 +86,34 @@
 
     barrier = pltpu.get_barrier_semaphore()
 
-    def greet(step, carry):
-        pl.semaphore_signal(barrier, inc=1, device_id=(sky, lax.rem(me + step, count)), device_id_type=MESH)
-        return carry
-
-    lax.fori_loop(1, count, greet, 0)
+    is_early = me < early_count
+
+    def signal(semaphore, first, wide):
+        def one(step, carry):
+            peer = lax.rem(me + step, count) if wide else first + step
+            pl.semaphore_signal(semaphore, inc=1, device_id=(sky, peer), device_id_type=MESH)
+            return carry
+
+        return one
+
+    @pl.when(is_early)
+    def _():
+        lax.fori_loop(1, count, signal(barrier, 0, True), 0)
+
+    @pl.when(jnp.logical_not(is_early))
+    def _():
+        lax.fori_loop(0, me - early_count, signal(barrier, early_count, False), 0)
+        lax.fori_loop(me - early_count + 1, late_count, signal(barrier, early_count, False), 0)
 
     for which in range(2):
         padded[which, :PAD] = jnp.zeros((PAD, BLK), jnp.float32)
         padded[which, PAD + second_rows * halves :] = jnp.zeros((PAD, BLK), jnp.float32)
     send[1] = jnp.zeros(send.shape[1:], jnp.float32)
+
+    @pl.when(jnp.logical_not(is_early))
+    def _():
+        pl.semaphore_wait(barrier, count - 1)
+        lax.fori_loop(0, early_count, signal(late_sem, 0, False), 0)
 
     loads[0].wait()
     series[...] = series_in[...].astype(jnp.float32)
@@ -140,7 +163,7 @@
         for which in (1, 0):
             shift = drift[0, (LEVELS + level) if which == 0 else (LEVELS - 1 - level)]
             channel = 2 * level + which
-            if blocks % 8 == 0:
+            if flat:
                 devices = pl.ds(first_device, half_count)
                 value = padded[which, pl.ds(PAD + first_device * blocks - shift, half_count * blocks), :]
                 send[channel, devices] = value.reshape(half_count, blocks, BLK) - send[1, devices]
@@ -158,22 +181,22 @@
             src_ref=source, dst_ref=target, send_sem=done, recv_sem=arrived, device_id=(sky, peer), device_id_type=MESH
         ).start()
 
-    def ship_far(channel):
+    def ship_far(channel, first=0, last=half_count, ascending=False):
         def one(step, carry):
-            peer = jnp.where(side == 0, count - 1 - step, step)
-            push(send.at[channel, peer], recv.at[channel, me], send_sem.at[channel], far_sem.at[channel], peer)
+            peer = jnp.where(side == 0, half_count + step if ascending else count - 1 - step, step)
+            push(send.at[channel, peer], recv.at[channel, slot(me)], send_sem.at[channel], far_sem.at[channel], peer)
             return carry
 
-        lax.fori_loop(0, half_count, one, 0)
+        lax.fori_loop(first, last, one, 0)
 
     def ship_near(channel):
         def one(step, carry):
             peer = near + lax.rem(place_in + step, half_count)
-            push(send.at[channel, peer], recv.at[channel, me], send_sem.at[channel], near_sem.at[channel], peer)
+            push(send.at[channel, peer], recv.at[channel, slot(me)], send_sem.at[channel], near_sem.at[channel], peer)
             return carry
 
         lax.fori_loop(1, half_count, one, 0)
-        pltpu.make_async_copy(send.at[channel, me], recv.at[channel, me], near_sem.at[channel]).start()
+        pltpu.make_async_copy(send.at[channel, me], recv.at[channel, slot(me)], near_sem.at[channel]).start()
 
     def ship_base():
         def one(step, carry):
@@ -206,14 +229,29 @@
         second_stage((1 - side) * (half_rows - HALO), half_rows + HALO)
         place(level, far)
 
+        @pl.when(jnp.logical_and(level == 0, is_early))
+        def _():
+            pl.semaphore_wait(barrier, early_count - 1)
+
         @pl.when(level == 0)
         def _():
-            pl.semaphore_wait(barrier, count - 1)
-
-        ship_far(2 * level)
+            ship_far(0, 0, half_count // 2, ascending=True)
+
+        @pl.when(jnp.logical_and(level == 0, side == 0))
+        def _():
+            pl.semaphore_wait(late_sem, late_count)
+
+        @pl.when(level == 0)
+        def _():
+            ship_far(0, half_count // 2, half_count, ascending=True)
+
+        @pl.when(jnp.logical_and(level == 0, jnp.logical_and(side == 1, is_early)))
+        def _():
+            pl.semaphore_wait(late_sem, late_count)
 
         @pl.when(level > 0)
         def _():
+            ship_far(2 * level)
             ship_far(2 * level + 1)
 
         second_stage(side * (half_rows + HALO), half_rows - HALO)
@@ -236,7 +274,7 @@
 
     lax.fori_loop(0, LEVELS, one_level, 0)
 
-    far_devices, near_devices = pl.ds(far, half_count), pl.ds(near, half_count)
+    far_devices, near_devices = span(far), span(near)
     await_bytes = lambda part, arrived: pltpu.make_async_copy(part, part, arrived).wait()
 
     channels = [channel for channel in range(KCOH) if channel != 1]
@@ -255,10 +293,9 @@
         await_bytes(recv.at[channel, near_devices], near_sem.at[channel])
         await_bytes(recv.at[channel, far_devices], far_sem.at[channel])
         line = step * 2 * count if isinstance(step, int) else pl.multiple_of(step * 2 * count, 2 * count)
-        arrived = recv.at[channel].reshape(count * blocks, BLK) if blocks % 8 == 0 else None
         for block in range(blocks):
-            if blocks % 8 == 0:
-                value = arrived[pl.ds(block, count, stride=blocks), :]
+            if flat:
+                value = recv[channel, pl.ds(block, count, stride=blocks), :]
             else:
                 value = recv[channel, :, block, :]
             high = value.astype(jnp.bfloat16)
@@ -273,7 +310,7 @@
     lax.fori_loop(0, KCOH - 2, stage_one, 0)
     await_bytes(recv.at[1, near_devices], near_sem.at[1])
     await_bytes(from_far, total_sem.at[1])
-    base = jnp.sum(recv[1, near_devices], axis=0) + from_far[...]
+    base = jnp.sum(recv[1, near_devices].reshape(half_count, blocks, BLK), axis=0) + from_far[...]
     early = (KCOH - 2) * 2 * count
     width = halves * BLK
     parts = blocks // halves
@@ -328,7 +365,7 @@
             pltpu.VMEM((4, 2, second_rows // 2 + HALO, first_rows), jnp.float32),
             pltpu.VMEM((2, points // BLK + 2 * PAD, BLK), jnp.float32),
             pltpu.VMEM((KCOH, count, blocks, BLK), jnp.float32),
-            pltpu.VMEM((KCOH, count, blocks, BLK), jnp.float32),
+            pltpu.VMEM((KCOH, count * blocks, BLK) if blocks % 8 == 0 else (KCOH, count, blocks, BLK), jnp.float32),
             pltpu.VMEM((count // 2, blocks, BLK), jnp.float32),
             pltpu.VMEM((blocks, BLK), jnp.float32),
             pltpu.VMEM((blocks, BLK), jnp.float32),
@@ -341,6 +378,7 @@
             pltpu.SemaphoreType.DMA((KCOH,)),
             pltpu.SemaphoreType.DMA,
             pltpu.SemaphoreType.DMA((2,)),
+            pltpu.SemaphoreType.REGULAR,
         ],
         compiler_params=pltpu.CompilerParams(
             collective_id=0, has_side_effects=True, vmem_limit_bytes=60 << 20

time: 38 us -> 38 us (level)
  no operation moved by 1% of the time
where the time goes in v4:
time: 38 us; the launch traced here: 37.8 us
  Pallas kernels  36.7 us (97%)
  other arithmetic  1.06 us (3%)
    pallas_call x1, Pallas kernels, local(): pl.pallas_call(functools.partial(kernel, count), out_shape=pltpu.VMEM((tr...  36.7 us
    div x1, other arithmetic, local(): return summed / segments  1.06 us

profile of v4, /device:TPU:0, one launch (start us, length us, event | category | flops | bytes accessed | tf_op | source)
XLA Modules:
  0.0 37.8 jit_solution(8062971177087168808)
XLA Ops:
  0.0 36.7 %shard_map.73 = f32[64,4096]{1,0:T(8,128)S(1)} custom-call(s32[1,6]{1,0:T(1,128)} %drift_hbm.1, bf16[1024,128]{1,0:T(8,128)(2,1)} %bitcast.12, f32[1024,128]{1,0:T(8,128)} %bitcast.11, f32[3,2,256,256]{3,2,1,0:T(8,128)} %constant.9.clone.chirp_hbm, f32[2,256,256]{2,1,0:T(8,128)} %constant.10.clone.twist_hbm, bf16[512,512]{1,0:T(8,128)(2,1)} %constant.11.clone.table_hbm, ...), custom_call_target="tpu_custom_call" | custom-call | tf_op jit(solution)/shard_map/pallas_call | solution.py:346
  36.7 1.1 %broadcast_multiply_fusion = f32[64,4096]{1,0:T(8,128)} fusion(f32[64,4096]{1,0:T(8,128)S(1)} %shard_map.73), kind=kLoop, calls=%fused_computation | loop fusion | flops 262144 | bytes 2097152 | tf_op jit(solution)/shard_map/div | solution.py:395

commit v5 on v4

--- a/solution.py
+++ b/solution.py
@@ -32,7 +32,7 @@
     second_rows = points // first_rows
     outer = np.arange(first_rows, dtype=np.int64)
     inner = np.arange(second_rows, dtype=np.int64)
-    angle = np.float32(2.0 * math.pi / points) * (outer[:, None] * inner[None, :] % points).astype(np.float32)
+    angle = np.float32(2.0 * math.pi / points) * (inner[:, None] * outer[None, :] % points).astype(np.float32)
     return np.stack([np.cos(angle), np.sin(angle)]).astype(np.float32)
 
 
@@ -41,7 +41,7 @@
     rate = (np.arange(LEVELS, KCOH, dtype=np.float32) - np.float32((KCOH - 1) / 2.0)) * np.float32(chirp_step)
     phases = (np.float32(2.0 * math.pi) * rate)[:, None] * (position * position)[None, :]
     both = np.stack([np.cos(phases), np.sin(phases)], 1).astype(np.float32)
-    return both.reshape(LEVELS, 2, first_rows, points // first_rows)
+    return np.swapaxes(both.reshape(LEVELS, 2, first_rows, points // first_rows), 2, 3).copy()
 
 
 def kernel(
@@ -51,15 +51,12 @@
     send, recv, gather, total_far, from_far, picks, staged,
     load_sem, chirp_sem, send_sem, far_sem, near_sem, gather_sem, total_sem, late_sem,
 ):
-    _, first_rows, second_rows = strain.shape
+    _, second_rows, first_rows = strain.shape
     halves = first_rows // BLK
     blocks = second_rows * halves // count
     half_count = count // 2
     early_count = half_count + half_count // 2
     late_count = count - early_count
-    flat = blocks % 8 == 0
-    slot = lambda device: pl.ds(pl.multiple_of(device * blocks, blocks), blocks) if flat else device
-    span = lambda device: pl.ds(pl.multiple_of(device * blocks, blocks), half_count * blocks) if flat else pl.ds(device, half_count)
     half_rows = second_rows // 2
     points = first_rows * second_rows
     sky = lax.axis_index("sky")
@@ -115,55 +112,79 @@
         pl.semaphore_wait(barrier, count - 1)
         lax.fori_loop(0, early_count, signal(late_sem, 0, False), 0)
 
+    pieces = second_rows // BLK
+
+    def turned(source, target):
+        for which in range(2):
+            for piece in range(pieces):
+                lines = pl.ds(2 * piece + which, first_rows, stride=2 * pieces)
+                target[which, piece * BLK : (piece + 1) * BLK, :] = source[lines, :].T
+
+    def demodulate(level):
+        for first in range(0, second_rows, HALO):
+            rows = slice(first, first + HALO)
+            chirp_cos, chirp_sin = chirp[level, 0, rows, :], chirp[level, 1, rows, :]
+            real, imag = strain[0, rows, :], strain[1, rows, :]
+            real_cos, imag_sin = real * chirp_cos, imag * chirp_sin
+            imag_cos, real_sin = imag * chirp_cos, real * chirp_sin
+            demods = ((real_cos + imag_sin, imag_cos - real_sin), (real_cos - imag_sin, imag_cos + real_sin))
+            for kind in range(2):
+                weight = weights[kind, rows, :]
+                for upper in range(2):
+                    start = (2 * upper + kind) * second_rows + first
+                    for part in range(2):
+                        lanes = slice((1 - part) * first_rows, (2 - part) * first_rows)
+                        weighted[start : start + HALO, lanes] = (weight * demods[upper][part]).astype(jnp.bfloat16)
+
     loads[0].wait()
     series[...] = series_in[...].astype(jnp.float32)
+    turned(series, strain)
     loads[1].wait()
-    pieces = second_rows // BLK
-    for which in range(2):
-        for piece in range(pieces):
-            lanes = slice(piece * BLK, (piece + 1) * BLK)
-            lines = pl.ds(2 * piece + which, first_rows, stride=2 * pieces)
-            strain[which, :, lanes] = series[lines, :]
-            weights[which, :, lanes] = antenna[lines, :]
-
-    weight_a, weight_b = weights[0], weights[1]
-    total = lambda value: jnp.sum(jnp.sum(value, axis=0, keepdims=True), axis=1, keepdims=True)
-    aa = total(weight_a * weight_a) / points + tiny_eps
-    bb = total(weight_b * weight_b) / points + tiny_eps
-    ab = total(weight_a * weight_b) / points
-    scale = 1.0 / (points * jnp.maximum(aa * bb - ab * ab, 0.1 * aa * bb))
-    coef_a, coef_b, coef_ab = bb * scale, aa * scale, 2.0 * ab * scale
+    turned(antenna, weights)
+    chirp_load(0).wait()
+    demodulate(0)
+
+    def coefficients():
+        sums = [0.0, 0.0, 0.0]
+        for first in range(0, second_rows, HALO):
+            rows = slice(first, first + HALO)
+            weight_a, weight_b = weights[0, rows, :], weights[1, rows, :]
+            sums = [held + value for held, value in zip(sums, (weight_a * weight_a, weight_b * weight_b, weight_a * weight_b))]
+        aa, bb, ab = [jnp.sum(jnp.sum(held, axis=0, keepdims=True), axis=1, keepdims=True) / points for held in sums]
+        aa, bb = aa + tiny_eps, bb + tiny_eps
+        scale = 1.0 / (points * jnp.maximum(aa * bb - ab * ab, 0.1 * aa * bb))
+        return bb * scale, aa * scale, 2.0 * ab * scale
 
     for load in loads[2:]:
         load.wait()
     for level in range(1, LEVELS):
         chirp_load(level).start()
 
-    def second_stage(start, size):
+    def second_stage(coefs, start, size):
+        coef_a, coef_b, coef_ab = coefs
         start = pl.multiple_of(start, HALO)
+        lines = jnp.concatenate([table[pl.ds(start, size), :], table[pl.ds(second_rows + start, size), :]], axis=0)
         for which in range(4):
-            for part in range(2):
-                spectra[which, part, :size] = lax.dot_general(
-                    table[pl.ds(part * second_rows + start, size), :], middle[which], (((1,), (1,)), ((), ())),
-                    preferred_element_type=jnp.float32,
+            spectra[which, : 2 * size] = jnp.dot(lines, middle[which], preferred_element_type=jnp.float32)
+        for which in range(2):
+            for first in range(0, size, HALO):
+                real_rows, imag_rows = slice(first, first + HALO), slice(size + first, size + first + HALO)
+                a_real, a_imag = spectra[2 * which, real_rows, :], spectra[2 * which, imag_rows, :]
+                b_real, b_imag = spectra[2 * which + 1, real_rows, :], spectra[2 * which + 1, imag_rows, :]
+                value = (
+                    coef_a * (a_real * a_real + a_imag * a_imag)
+                    + coef_b * (b_real * b_real + b_imag * b_imag)
+                    - coef_ab * (a_real * b_real + a_imag * b_imag)
                 )
-        for which in range(2):
-            a_real, a_imag = spectra[2 * which, 0, :size], spectra[2 * which, 1, :size]
-            b_real, b_imag = spectra[2 * which + 1, 0, :size], spectra[2 * which + 1, 1, :size]
-            value = (
-                coef_a * (a_real * a_real + a_imag * a_imag)
-                + coef_b * (b_real * b_real + b_imag * b_imag)
-                - coef_ab * (a_real * b_real + a_imag * b_imag)
-            )
-            for half in range(halves):
-                lines = pl.ds(PAD + halves * start + half, size, stride=halves)
-                padded[which, lines, :] = value[:, half * BLK : (half + 1) * BLK]
+                for half in range(halves):
+                    lines = pl.ds(PAD + halves * (start + first) + half, HALO, stride=halves)
+                    padded[which, lines, :] = value[:, half * BLK : (half + 1) * BLK]
 
     def place(level, first_device):
         for which in (1, 0):
             shift = drift[0, (LEVELS + level) if which == 0 else (LEVELS - 1 - level)]
             channel = 2 * level + which
-            if flat:
+            if blocks % 8 == 0:
                 devices = pl.ds(first_device, half_count)
                 value = padded[which, pl.ds(PAD + first_device * blocks - shift, half_count * blocks), :]
                 send[channel, devices] = value.reshape(half_count, blocks, BLK) - send[1, devices]
@@ -184,7 +205,7 @@
     def ship_far(channel, first=0, last=half_count, ascending=False):
         def one(step, carry):
             peer = jnp.where(side == 0, half_count + step if ascending else count - 1 - step, step)
-            push(send.at[channel, peer], recv.at[channel, slot(me)], send_sem.at[channel], far_sem.at[channel], peer)
+            push(send.at[channel, peer], recv.at[channel, :, me], send_sem.at[channel], far_sem.at[channel], peer)
             return carry
 
         lax.fori_loop(first, last, one, 0)
@@ -192,11 +213,11 @@
     def ship_near(channel):
         def one(step, carry):
             peer = near + lax.rem(place_in + step, half_count)
-            push(send.at[channel, peer], recv.at[channel, slot(me)], send_sem.at[channel], near_sem.at[channel], peer)
+            push(send.at[channel, peer], recv.at[channel, :, me], send_sem.at[channel], near_sem.at[channel], peer)
             return carry
 
         lax.fori_loop(1, half_count, one, 0)
-        pltpu.make_async_copy(send.at[channel, me], recv.at[channel, slot(me)], near_sem.at[channel]).start()
+        pltpu.make_async_copy(send.at[channel, me], recv.at[channel, :, me], near_sem.at[channel]).start()
 
     def ship_base():
         def one(step, carry):
@@ -208,25 +229,20 @@
         pltpu.make_async_copy(send.at[1, mirror], gather.at[place_in], gather_sem).start()
 
     def one_level(level, carry):
-        chirp_load(level).wait()
-        chirp_cos, chirp_sin = chirp[level, 0], chirp[level, 1]
-        real, imag = strain[0], strain[1]
-        real_cos, imag_sin = real * chirp_cos, imag * chirp_sin
-        imag_cos, real_sin = imag * chirp_cos, real * chirp_sin
-        demods = ((real_cos + imag_sin, imag_cos - real_sin), (real_cos - imag_sin, imag_cos + real_sin))
+        spread[...] = jnp.dot(weighted[...], table[...], preferred_element_type=jnp.float32)
+        coefs = coefficients()
         for which in range(4):
-            weight = weights[which % 2]
-            for part in range(2):
-                lines = slice(part * first_rows, (part + 1) * first_rows)
-                weighted[which, lines, :] = (weight * demods[which // 2][part]).astype(jnp.bfloat16)
-        twist_cos, twist_sin = twist[0], twist[1]
-        for which in range(4):
-            spread[which] = jnp.dot(table[...], weighted[which], preferred_element_type=jnp.float32)
-            one_real, one_imag = spread[which, :first_rows], spread[which, first_rows:]
-            middle[which, :, :second_rows] = (one_real * twist_cos + one_imag * twist_sin).astype(jnp.bfloat16)
-            middle[which, :, second_rows:] = (one_imag * twist_cos - one_real * twist_sin).astype(jnp.bfloat16)
-
-        second_stage((1 - side) * (half_rows - HALO), half_rows + HALO)
+            for first in range(0, second_rows, HALO):
+                rows = slice(first, first + HALO)
+                lines = slice(which * second_rows + first, which * second_rows + first + HALO)
+                twist_cos, twist_sin = twist[0, rows, :], twist[1, rows, :]
+                one_imag, one_real = spread[lines, :first_rows], spread[lines, first_rows:]
+                middle[which, first : first + HALO, :] = (one_real * twist_cos + one_imag * twist_sin).astype(jnp.bfloat16)
+                middle[which, second_rows + first : second_rows + first + HALO, :] = (
+                    one_imag * twist_cos - one_real * twist_sin
+                ).astype(jnp.bfloat16)
+
+        second_stage(coefs, (1 - side) * (half_rows - HALO), half_rows + HALO)
         place(level, far)
 
         @pl.when(jnp.logical_and(level == 0, is_early))
@@ -254,7 +270,7 @@
             ship_far(2 * level)
             ship_far(2 * level + 1)
 
-        second_stage(side * (half_rows + HALO), half_rows - HALO)
+        second_stage(coefs, side * (half_rows + HALO), half_rows - HALO)
         place(level, near)
 
         @pl.when(level == 0)
@@ -270,11 +286,16 @@
             total_far[...] = jnp.sum(gather[...], axis=0)
             push(total_far, from_far, total_sem.at[0], total_sem.at[1], mirror)
 
+        @pl.when(level < LEVELS - 1)
+        def _():
+            chirp_load(level + 1).wait()
+            demodulate(level + 1)
+
         return carry
 
     lax.fori_loop(0, LEVELS, one_level, 0)
 
-    far_devices, near_devices = span(far), span(near)
+    far_devices, near_devices = pl.ds(pl.multiple_of(far, half_count), half_count), pl.ds(pl.multiple_of(near, half_count), half_count)
     await_bytes = lambda part, arrived: pltpu.make_async_copy(part, part, arrived).wait()
 
     channels = [channel for channel in range(KCOH) if channel != 1]
@@ -290,14 +311,11 @@
     ).astype(jnp.bfloat16)
 
     def stage(step, channel):
-        await_bytes(recv.at[channel, near_devices], near_sem.at[channel])
-        await_bytes(recv.at[channel, far_devices], far_sem.at[channel])
+        await_bytes(recv.at[channel, :, near_devices], near_sem.at[channel])
+        await_bytes(recv.at[channel, :, far_devices], far_sem.at[channel])
         line = step * 2 * count if isinstance(step, int) else pl.multiple_of(step * 2 * count, 2 * count)
         for block in range(blocks):
-            if flat:
-                value = recv[channel, pl.ds(block, count, stride=blocks), :]
-            else:
-                value = recv[channel, :, block, :]
+            value = recv[channel, block]
             high = value.astype(jnp.bfloat16)
             lanes = slice(block * BLK, (block + 1) * BLK)
             staged[pl.ds(line, count), lanes] = high
@@ -308,9 +326,9 @@
         return carry
 
     lax.fori_loop(0, KCOH - 2, stage_one, 0)
-    await_bytes(recv.at[1, near_devices], near_sem.at[1])
+    await_bytes(recv.at[1, :, near_devices], near_sem.at[1])
     await_bytes(from_far, total_sem.at[1])
-    base = jnp.sum(recv[1, near_devices].reshape(half_count, blocks, BLK), axis=0) + from_far[...]
+    base = jnp.sum(recv[1, :, near_devices], axis=1) + from_far[...]
     early = (KCOH - 2) * 2 * count
     width = halves * BLK
     parts = blocks // halves
@@ -354,18 +372,18 @@
             pltpu.VMEM(block, jnp.float32),
             pltpu.VMEM(block, jnp.float32),
             pltpu.VMEM(chirps.shape, jnp.float32),
-            pltpu.VMEM((2, first_rows, second_rows), jnp.float32),
+            pltpu.VMEM((2, second_rows, first_rows), jnp.float32),
             pltpu.VMEM((2 * first_rows, 2 * first_rows), jnp.bfloat16),
             pltpu.VMEM((segments, tracks.shape[0]), jnp.int32),
-            pltpu.VMEM((2, first_rows, second_rows), jnp.float32),
-            pltpu.VMEM((2, first_rows, second_rows), jnp.float32),
-            pltpu.VMEM((4, 2 * first_rows, second_rows), jnp.bfloat16),
-            pltpu.VMEM((4, 2 * first_rows, second_rows), jnp.float32),
-            pltpu.VMEM((4, first_rows, 2 * second_rows), jnp.bfloat16),
-            pltpu.VMEM((4, 2, second_rows // 2 + HALO, first_rows), jnp.float32),
+            pltpu.VMEM((2, second_rows, first_rows), jnp.float32),
+            pltpu.VMEM((2, second_rows, first_rows), jnp.float32),
+            pltpu.VMEM((4 * second_rows, 2 * first_rows), jnp.bfloat16),
+            pltpu.VMEM((4 * second_rows, 2 * first_rows), jnp.float32),
+            pltpu.VMEM((4, 2 * second_rows, first_rows), jnp.bfloat16),
+            pltpu.VMEM((4, second_rows + 2 * HALO, first_rows), jnp.float32),
             pltpu.VMEM((2, points // BLK + 2 * PAD, BLK), jnp.float32),
             pltpu.VMEM((KCOH, count, blocks, BLK), jnp.float32),
-            pltpu.VMEM((KCOH, count * blocks, BLK) if blocks % 8 == 0 else (KCOH, count, blocks, BLK), jnp.float32),
+            pltpu.VMEM((KCOH, blocks, count, BLK), jnp.float32),
             pltpu.VMEM((count // 2, blocks, BLK), jnp.float32),
             pltpu.VMEM((blocks, BLK), jnp.float32),
             pltpu.VMEM((blocks, BLK), jnp.float32),

time: 38 us -> 37.5 us (0.987)
  Pallas kernels: 36.7 us -> 36.3 us
where the time goes in v5:
time: 37.5 us; the launch traced here: 37.4 us
  Pallas kernels  36.3 us (97%)
  other arithmetic  1.06 us (3%)
    pallas_call x1, Pallas kernels, local(): pl.pallas_call(functools.partial(kernel, count), out_shape=pltpu.VMEM((tr...  36.3 us
    div x1, other arithmetic, local(): return summed / segments  1.06 us

profile of v5, /device:TPU:0, one launch (start us, length us, event | category | flops | bytes accessed | tf_op | source)
XLA Modules:
  0.0 37.4 jit_solution(3057310903009277063)
XLA Ops:
  0.0 36.3 %shard_map.73 = f32[64,4096]{1,0:T(8,128)S(1)} custom-call(s32[1,6]{1,0:T(1,128)} %drift_hbm.1, bf16[1024,128]{1,0:T(8,128)(2,1)} %bitcast.12, f32[1024,128]{1,0:T(8,128)} %bitcast.11, f32[3,2,256,256]{3,2,1,0:T(8,128)} %constant.9.clone.chirp_hbm, f32[2,256,256]{2,1,0:T(8,128)} %constant.10.clone.twist_hbm, bf16[512,512]{1,0:T(8,128)(2,1)} %constant.11.clone.table_hbm, ...), custom_call_target="tpu_custom_call" | custom-call | tf_op jit(solution)/shard_map/pallas_call | solution.py:364
  36.3 1.1 %broadcast_multiply_fusion = f32[64,4096]{1,0:T(8,128)} fusion(f32[64,4096]{1,0:T(8,128)S(1)} %shard_map.73), kind=kLoop, calls=%fused_computation | loop fusion | flops 262144 | bytes 2097152 | tf_op jit(solution)/shard_map/div | solution.py:413

commit v6 on v5

--- a/solution.py
+++ b/solution.py
@@ -265,20 +265,20 @@
         def _():
             pl.semaphore_wait(late_sem, late_count)
 
+        second_stage(coefs, side * (half_rows + HALO), half_rows - HALO)
+        place(level, near)
+
+        @pl.when(level == 0)
+        def _():
+            ship_base()
+
+        ship_near(2 * level + 1)
+        ship_near(2 * level)
+
         @pl.when(level > 0)
         def _():
             ship_far(2 * level)
             ship_far(2 * level + 1)
-
-        second_stage(coefs, side * (half_rows + HALO), half_rows - HALO)
-        place(level, near)
-
-        @pl.when(level == 0)
-        def _():
-            ship_base()
-
-        ship_near(2 * level + 1)
-        ship_near(2 * level)
 
         @pl.when(level == LEVELS - 2)
         def _():

time: 37.5 us -> 37.5 us (level)
  no operation moved by 1% of the time
where the time goes in v6:
time: 37.5 us; the launch traced here: 37.4 us
  Pallas kernels  36.3 us (97%)
  other arithmetic  1.06 us (3%)
    pallas_call x1, Pallas kernels, local(): pl.pallas_call(functools.partial(kernel, count), out_shape=pltpu.VMEM((tr...  36.3 us
    div x1, other arithmetic, local(): return summed / segments  1.06 us

profile of v6, /device:TPU:0, one launch (start us, length us, event | category | flops | bytes accessed | tf_op | source)
XLA Modules:
  0.0 37.4 jit_solution(4878739826716287799)
XLA Ops:
  0.0 36.3 %shard_map.73 = f32[64,4096]{1,0:T(8,128)S(1)} custom-call(s32[1,6]{1,0:T(1,128)} %drift_hbm.1, bf16[1024,128]{1,0:T(8,128)(2,1)} %bitcast.12, f32[1024,128]{1,0:T(8,128)} %bitcast.11, f32[3,2,256,256]{3,2,1,0:T(8,128)} %constant.9.clone.chirp_hbm, f32[2,256,256]{2,1,0:T(8,128)} %constant.10.clone.twist_hbm, bf16[512,512]{1,0:T(8,128)(2,1)} %constant.11.clone.table_hbm, ...), custom_call_target="tpu_custom_call" | custom-call | tf_op jit(solution)/shard_map/pallas_call | solution.py:364
  36.3 1.1 %broadcast_multiply_fusion = f32[64,4096]{1,0:T(8,128)} fusion(f32[64,4096]{1,0:T(8,128)S(1)} %shard_map.73), kind=kLoop, calls=%fused_computation | loop fusion | flops 262144 | bytes 2097152 | tf_op jit(solution)/shard_map/div | solution.py:413

commit v7 on v6

--- a/solution.py
+++ b/solution.py
@@ -202,27 +202,29 @@
             src_ref=source, dst_ref=target, send_sem=done, recv_sem=arrived, device_id=(sky, peer), device_id_type=MESH
         ).start()
 
-    def ship_far(channel, first=0, last=half_count, ascending=False):
+    def ship_far(level, channels, first=0, last=half_count, ascending=False):
         def one(step, carry):
             peer = jnp.where(side == 0, half_count + step if ascending else count - 1 - step, step)
-            push(send.at[channel, peer], recv.at[channel, :, me], send_sem.at[channel], far_sem.at[channel], peer)
+            push(send.at[channels, peer], recv.at[channels, :, me], send_sem.at[level], far_sem.at[level], peer)
             return carry
 
         lax.fori_loop(first, last, one, 0)
 
-    def ship_near(channel):
+    def ship_near(level):
+        channels = pl.ds(2 * level, 2)
+
         def one(step, carry):
             peer = near + lax.rem(place_in + step, half_count)
-            push(send.at[channel, peer], recv.at[channel, :, me], send_sem.at[channel], near_sem.at[channel], peer)
+            push(send.at[channels, peer], recv.at[channels, :, me], send_sem.at[LEVELS + level], near_sem.at[level], peer)
             return carry
 
         lax.fori_loop(1, half_count, one, 0)
-        pltpu.make_async_copy(send.at[channel, me], recv.at[channel, :, me], near_sem.at[channel]).start()
+        pltpu.make_async_copy(send.at[channels, me], recv.at[channels, :, me], near_sem.at[level]).start()
 
     def ship_base():
         def one(step, carry):
             other = lax.rem(place_in + step, half_count)
-            push(send.at[1, far + other], gather.at[place_in], send_sem.at[1], gather_sem, near + other)
+            push(send.at[1, far + other], gather.at[place_in], send_sem.at[2 * LEVELS], gather_sem, near + other)
             return carry
 
         lax.fori_loop(1, half_count, one, 0)
@@ -251,7 +253,7 @@
 
         @pl.when(level == 0)
         def _():
-            ship_far(0, 0, half_count // 2, ascending=True)
+            ship_far(0, pl.ds(0, 1), 0, half_count // 2, ascending=True)
 
         @pl.when(jnp.logical_and(level == 0, side == 0))
         def _():
@@ -259,7 +261,7 @@
 
         @pl.when(level == 0)
         def _():
-            ship_far(0, half_count // 2, half_count, ascending=True)
+            ship_far(0, pl.ds(0, 1), half_count // 2, half_count, ascending=True)
 
         @pl.when(jnp.logical_and(level == 0, jnp.logical_and(side == 1, is_early)))
         def _():
@@ -272,13 +274,11 @@
         def _():
             ship_base()
 
-        ship_near(2 * level + 1)
-        ship_near(2 * level)
+        ship_near(level)
 
         @pl.when(level > 0)
         def _():
-            ship_far(2 * level)
-            ship_far(2 * level + 1)
+            ship_far(level, pl.ds(2 * level, 2))
 
         @pl.when(level == LEVELS - 2)
         def _():
@@ -310,26 +310,28 @@
         jnp.where(same, 1.0, 0.0).astype(jnp.bfloat16), chosen, (((1,), (1,)), ((), ())), preferred_element_type=jnp.float32
     ).astype(jnp.bfloat16)
 
+    def arrive(level):
+        pair = pl.ds(2 * level, 2)
+        await_bytes(recv.at[pair, :, near_devices], near_sem.at[level])
+        await_bytes(recv.at[pair if level else pl.ds(0, 1), :, far_devices], far_sem.at[level])
+
     def stage(step, channel):
-        await_bytes(recv.at[channel, :, near_devices], near_sem.at[channel])
-        await_bytes(recv.at[channel, :, far_devices], far_sem.at[channel])
-        line = step * 2 * count if isinstance(step, int) else pl.multiple_of(step * 2 * count, 2 * count)
+        line = step * 2 * count
         for block in range(blocks):
             value = recv[channel, block]
             high = value.astype(jnp.bfloat16)
             lanes = slice(block * BLK, (block + 1) * BLK)
-            staged[pl.ds(line, count), lanes] = high
-            staged[pl.ds(line + count, count), lanes] = (value - high.astype(jnp.float32)).astype(jnp.bfloat16)
-
-    def stage_one(step, carry):
-        stage(step, jnp.where(step == 0, 0, step + 1))
-        return carry
-
-    lax.fori_loop(0, KCOH - 2, stage_one, 0)
-    await_bytes(recv.at[1, :, near_devices], near_sem.at[1])
+            staged[line : line + count, lanes] = high
+            staged[line + count : line + 2 * count, lanes] = (value - high.astype(jnp.float32)).astype(jnp.bfloat16)
+
+    for level in range(LEVELS - 1):
+        arrive(level)
+        for step, channel in enumerate(channels):
+            if channel // 2 == level:
+                stage(step, channel)
     await_bytes(from_far, total_sem.at[1])
     base = jnp.sum(recv[1, :, near_devices], axis=1) + from_far[...]
-    early = (KCOH - 2) * 2 * count
+    early = (KCOH - 3) * 2 * count
     width = halves * BLK
     parts = blocks // halves
     for part in range(parts):
@@ -338,17 +340,18 @@
         out_ref[:, columns] = line + jnp.dot(
             picks[:, :early], staged[:early, columns], preferred_element_type=jnp.float32
         )
-    stage(KCOH - 2, channels[-1])
+    arrive(LEVELS - 1)
+    for step in (KCOH - 3, KCOH - 2):
+        stage(step, channels[step])
     for part in range(parts):
         columns = slice(part * width, (part + 1) * width)
         out_ref[:, columns] += jnp.dot(picks[:, early:], staged[early:, columns], preferred_element_type=jnp.float32)
 
-    for channel in range(KCOH):
-        if channel == 1:
-            part = send.at[1, pl.ds(0, 2 * (half_count - 1))]
-        else:
-            part = send.at[channel, pl.ds(0, count - 1)]
-        await_bytes(part, send_sem.at[channel])
+    for level in range(LEVELS):
+        pair = pl.ds(2 * level, 2)
+        await_bytes(send.at[pair if level else pl.ds(0, 1), pl.ds(0, half_count)], send_sem.at[level])
+        await_bytes(send.at[pair, pl.ds(0, half_count - 1)], send_sem.at[LEVELS + level])
+    await_bytes(send.at[1, pl.ds(0, half_count - 1)], send_sem.at[2 * LEVELS])
     await_bytes(total_far, total_sem.at[0])
 
 
@@ -391,9 +394,9 @@
             pltpu.VMEM(((KCOH - 1) * 2 * count, points // count), jnp.bfloat16),
             pltpu.SemaphoreType.DMA((6,)),
             pltpu.SemaphoreType.DMA((LEVELS,)),
-            pltpu.SemaphoreType.DMA((KCOH,)),
-            pltpu.SemaphoreType.DMA((KCOH,)),
-            pltpu.SemaphoreType.DMA((KCOH,)),
+            pltpu.SemaphoreType.DMA((2 * LEVELS + 1,)),
+            pltpu.SemaphoreType.DMA((LEVELS,)),
+            pltpu.SemaphoreType.DMA((LEVELS,)),
             pltpu.SemaphoreType.DMA,
             pltpu.SemaphoreType.DMA((2,)),
             pltpu.SemaphoreType.REGULAR,

time: 37.5 us -> 36 us (0.960)
  the two profiles are of different devices: /device:TPU:0 before, /device:TPU:11 now
where the time goes in v7:
time: 36 us; the launch traced here: 35.9 us
  Pallas kernels  34.8 us (97%)
  other arithmetic  1.06 us (3%)
    pallas_call x1, Pallas kernels, local(): pl.pallas_call(functools.partial(kernel, count), out_shape=pltpu.VMEM((tr...  34.8 us
    div x1, other arithmetic, local(): return summed / segments  1.06 us

profile of v7, /device:TPU:11, one launch (start us, length us, event | category | flops | bytes accessed | tf_op | source)
XLA Modules:
  0.0 35.9 jit_solution(11523425533195005638)
XLA Ops:
  0.0 34.8 %shard_map.73 = f32[64,4096]{1,0:T(8,128)S(1)} custom-call(s32[1,6]{1,0:T(1,128)} %drift_hbm.1, bf16[1024,128]{1,0:T(8,128)(2,1)} %bitcast.12, f32[1024,128]{1,0:T(8,128)} %bitcast.11, f32[3,2,256,256]{3,2,1,0:T(8,128)} %constant.9.clone.chirp_hbm, f32[2,256,256]{2,1,0:T(8,128)} %constant.10.clone.twist_hbm, bf16[512,512]{1,0:T(8,128)(2,1)} %constant.11.clone.table_hbm, ...), custom_call_target="tpu_custom_call" | custom-call | tf_op jit(solution)/shard_map/pallas_call | solution.py:367
  34.8 1.1 %broadcast_multiply_fusion = f32[64,4096]{1,0:T(8,128)} fusion(f32[64,4096]{1,0:T(8,128)S(1)} %shard_map.73), kind=kLoop, calls=%fused_computation | loop fusion | flops 262144 | bytes 2097152 | tf_op jit(solution)/shard_map/div | solution.py:416

commit v8 on v7

--- a/solution.py
+++ b/solution.py
@@ -180,14 +180,14 @@
                     lines = pl.ds(PAD + halves * (start + first) + half, HALO, stride=halves)
                     padded[which, lines, :] = value[:, half * BLK : (half + 1) * BLK]
 
-    def place(level, first_device):
+    def place(level, first_device, devices_here):
         for which in (1, 0):
             shift = drift[0, (LEVELS + level) if which == 0 else (LEVELS - 1 - level)]
             channel = 2 * level + which
             if blocks % 8 == 0:
-                devices = pl.ds(first_device, half_count)
-                value = padded[which, pl.ds(PAD + first_device * blocks - shift, half_count * blocks), :]
-                send[channel, devices] = value.reshape(half_count, blocks, BLK) - send[1, devices]
+                devices = pl.ds(first_device, devices_here)
+                value = padded[which, pl.ds(PAD + first_device * blocks - shift, devices_here * blocks), :]
+                send[channel, devices] = value.reshape(devices_here, blocks, BLK) - send[1, devices]
             else:
                 def one(step, carry, which=which, channel=channel, shift=shift):
                     peer = first_device + step
@@ -195,7 +195,7 @@
                     send[channel, peer] = value - send[1, peer]
                     return carry
 
-                lax.fori_loop(0, half_count, one, 0)
+                lax.fori_loop(0, devices_here, one, 0)
 
     def push(source, target, done, arrived, peer):
         pltpu.make_async_remote_copy(
@@ -204,7 +204,7 @@
 
     def ship_far(level, channels, first=0, last=half_count, ascending=False):
         def one(step, carry):
-            peer = jnp.where(side == 0, half_count + step if ascending else count - 1 - step, step)
+            peer = jnp.where(side == 0, half_count + (step if ascending else lax.rem(step + half_count // 2, half_count)), step)
             push(send.at[channels, peer], recv.at[channels, :, me], send_sem.at[level], far_sem.at[level], peer)
             return carry
 
@@ -244,8 +244,10 @@
                     one_imag * twist_cos - one_real * twist_sin
                 ).astype(jnp.bfloat16)
 
-        second_stage(coefs, (1 - side) * (half_rows - HALO), half_rows + HALO)
-        place(level, far)
+        first_row = (1 - side) * (half_rows - HALO)
+        first_size = half_rows // 2 + 2 * HALO
+        second_stage(coefs, first_row, first_size)
+        place(level, far, half_count // 2)
 
         @pl.when(jnp.logical_and(level == 0, is_early))
         def _():
@@ -255,6 +257,9 @@
         def _():
             ship_far(0, pl.ds(0, 1), 0, half_count // 2, ascending=True)
 
+        second_stage(coefs, first_row + first_size, half_rows + HALO - first_size)
+        place(level, far + half_count // 2, half_count // 2)
+
         @pl.when(jnp.logical_and(level == 0, side == 0))
         def _():
             pl.semaphore_wait(late_sem, late_count)
@@ -268,7 +273,7 @@
             pl.semaphore_wait(late_sem, late_count)
 
         second_stage(coefs, side * (half_rows + HALO), half_rows - HALO)
-        place(level, near)
+        place(level, near, half_count)
 
         @pl.when(level == 0)
         def _():
@@ -341,11 +346,16 @@
             picks[:, :early], staged[:early, columns], preferred_element_type=jnp.float32
         )
     arrive(LEVELS - 1)
-    for step in (KCOH - 3, KCOH - 2):
-        stage(step, channels[step])
     for part in range(parts):
         columns = slice(part * width, (part + 1) * width)
-        out_ref[:, columns] += jnp.dot(picks[:, early:], staged[early:, columns], preferred_element_type=jnp.float32)
+        lines = []
+        for channel in channels[-2:]:
+            value = jnp.concatenate([recv[channel, part * halves + half] for half in range(halves)], axis=1)
+            high = value.astype(jnp.bfloat16)
+            lines += [high, (value - high.astype(jnp.float32)).astype(jnp.bfloat16)]
+        out_ref[:, columns] += jnp.dot(
+            picks[:, early:], jnp.concatenate(lines, axis=0), preferred_element_type=jnp.float32
+        )
 
     for level in range(LEVELS):
         pair = pl.ds(2 * level, 2)
@@ -391,7 +401,7 @@
             pltpu.VMEM((blocks, BLK), jnp.float32),
             pltpu.VMEM((blocks, BLK), jnp.float32),
             pltpu.VMEM((tracks.shape[0], (KCOH - 1) * 2 * count), jnp.bfloat16),
-            pltpu.VMEM(((KCOH - 1) * 2 * count, points // count), jnp.bfloat16),
+            pltpu.VMEM(((KCOH - 3) * 2 * count, points // count), jnp.bfloat16),
             pltpu.SemaphoreType.DMA((6,)),
             pltpu.SemaphoreType.DMA((LEVELS,)),
             pltpu.SemaphoreType.DMA((2 * LEVELS + 1,)),

time: 36 us -> 35.9 us (level)
  no operation moved by 1% of the time
where the time goes in v8:
time: 35.9 us; the launch traced here: 35.7 us
  Pallas kernels  34.7 us (97%)
  other arithmetic  1.06 us (3%)
    pallas_call x1, Pallas kernels, local(): pl.pallas_call(functools.partial(kernel, count), out_shape=pltpu.VMEM((tr...  34.7 us
    div x1, other arithmetic, local(): return summed / segments  1.06 us

profile of v8, /device:TPU:11, one launch (start us, length us, event | category | flops | bytes accessed | tf_op | source)
XLA Modules:
  0.0 35.7 jit_solution(8740468607640869958)
XLA Ops:
  0.0 34.7 %shard_map.73 = f32[64,4096]{1,0:T(8,128)S(1)} custom-call(s32[1,6]{1,0:T(1,128)} %drift_hbm.1, bf16[1024,128]{1,0:T(8,128)(2,1)} %bitcast.12, f32[1024,128]{1,0:T(8,128)} %bitcast.11, f32[3,2,256,256]{3,2,1,0:T(8,128)} %constant.9.clone.chirp_hbm, f32[2,256,256]{2,1,0:T(8,128)} %constant.10.clone.twist_hbm, bf16[512,512]{1,0:T(8,128)(2,1)} %constant.11.clone.table_hbm, ...), custom_call_target="tpu_custom_call" | custom-call | tf_op jit(solution)/shard_map/pallas_call | solution.py:377
  34.7 1.1 %broadcast_multiply_fusion = f32[64,4096]{1,0:T(8,128)} fusion(f32[64,4096]{1,0:T(8,128)S(1)} %shard_map.73), kind=kLoop, calls=%fused_computation | loop fusion | flops 262144 | bytes 2097152 | tf_op jit(solution)/shard_map/div | solution.py:426

commit v9 on v8

--- a/solution.py
+++ b/solution.py
@@ -15,6 +15,7 @@
 LEVELS = KCOH // 2
 PAD = 8
 HALO = 16
+SUB = 8
 MESH = pl.DeviceIdType.MESH
 
 chirp_step = 3.0
@@ -28,11 +29,11 @@
     return np.block([[cos, sin], [-sin, cos]]).astype(jnp.bfloat16)
 
 
-def twist_table(points, first_rows):
+def twist_factors(points, first_rows):
     second_rows = points // first_rows
+    inner = np.concatenate([SUB * np.arange(second_rows // SUB, dtype=np.int64), np.arange(SUB, dtype=np.int64)])
     outer = np.arange(first_rows, dtype=np.int64)
-    inner = np.arange(second_rows, dtype=np.int64)
-    angle = np.float32(2.0 * math.pi / points) * (inner[:, None] * outer[None, :] % points).astype(np.float32)
+    angle = (2.0 * math.pi / points) * (inner[:, None] * outer[None, :] % points).astype(np.float64)
     return np.stack([np.cos(angle), np.sin(angle)]).astype(np.float32)
 
 
@@ -45,10 +46,10 @@
 
 
 def kernel(
-    count, drift_hbm, series_hbm, antenna_hbm, chirp_hbm, twist_hbm, table_hbm, tracks_hbm, out_ref,
-    drift, series_in, series, antenna, chirp, twist, table, tracks,
+    count, drift_hbm, series_hbm, antenna_hbm, chirp_hbm, factors_hbm, table_hbm, tracks_hbm, out_ref,
+    drift, series_in, series, antenna, chirp, factors, twist, table, tracks,
     strain, weights, weighted, spread, middle, spectra, padded,
-    send, recv, gather, total_far, from_far, picks, staged,
+    send, recv, gather, total_far, from_far, picks, last_picks, staged,
     load_sem, chirp_sem, send_sem, far_sem, near_sem, gather_sem, total_sem, late_sem,
 ):
     _, second_rows, first_rows = strain.shape
@@ -70,16 +71,17 @@
     loads = [
         pltpu.make_async_copy(source, target, load_sem.at[index])
         for index, (source, target) in enumerate([
-            (series_hbm, series_in), (antenna_hbm, antenna), (table_hbm, table), (twist_hbm, twist), (drift_hbm, drift),
+            (series_hbm, series_in), (antenna_hbm, antenna), (table_hbm, table), (factors_hbm, factors), (drift_hbm, drift),
             (tracks_hbm, tracks),
         ])
     ]
     chirp_load = lambda level: pltpu.make_async_copy(chirp_hbm.at[level], chirp.at[level], chirp_sem.at[level])
     loads[0].start()
+    loads[3].start()
     loads[1].start()
     chirp_load(0).start()
-    for load in loads[2:]:
-        load.start()
+    for index in (4, 2, 5):
+        loads[index].start()
 
     barrier = pltpu.get_barrier_semaphore()
 
@@ -138,7 +140,14 @@
 
     loads[0].wait()
     series[...] = series_in[...].astype(jnp.float32)
+    loads[3].wait()
     turned(series, strain)
+    steps = second_rows // SUB
+    step_cos, step_sin = factors[0, steps:, :], factors[1, steps:, :]
+    for step in range(steps):
+        base_cos, base_sin = factors[0, step : step + 1, :], factors[1, step : step + 1, :]
+        twist[0, step * SUB : (step + 1) * SUB, :] = base_cos * step_cos - base_sin * step_sin
+        twist[1, step * SUB : (step + 1) * SUB, :] = base_sin * step_cos + base_cos * step_sin
     loads[1].wait()
     turned(antenna, weights)
     chirp_load(0).wait()
@@ -155,8 +164,8 @@
         scale = 1.0 / (points * jnp.maximum(aa * bb - ab * ab, 0.1 * aa * bb))
         return bb * scale, aa * scale, 2.0 * ab * scale
 
-    for load in loads[2:]:
-        load.wait()
+    loads[4].wait()
+    loads[2].wait()
     for level in range(1, LEVELS):
         chirp_load(level).start()
 
@@ -304,16 +313,18 @@
     await_bytes = lambda part, arrived: pltpu.make_async_copy(part, part, arrived).wait()
 
     channels = [channel for channel in range(KCOH) if channel != 1]
-    chosen = []
-    for channel in channels:
-        rate = LEVELS + channel // 2 if channel % 2 == 0 else LEVELS - 1 - channel // 2
-        chosen += [jnp.where(tracks[...] == rate, 1.0, 0.0).astype(jnp.bfloat16)] * 2
-    chosen = jnp.concatenate(chosen, axis=0)
     names = tracks.shape[1]
     same = lax.broadcasted_iota(jnp.int32, (names, names), 0) == lax.broadcasted_iota(jnp.int32, (names, names), 1)
-    picks[...] = lax.dot_general(
-        jnp.where(same, 1.0, 0.0).astype(jnp.bfloat16), chosen, (((1,), (1,)), ((), ())), preferred_element_type=jnp.float32
-    ).astype(jnp.bfloat16)
+    loads[5].wait()
+    for target, group in ((picks, channels[:-2]), (last_picks, channels[-2:])):
+        chosen = []
+        for channel in group:
+            rate = LEVELS + channel // 2 if channel % 2 == 0 else LEVELS - 1 - channel // 2
+            chosen += [jnp.where(tracks[...] == rate, 1.0, 0.0).astype(jnp.bfloat16)] * 2
+        target[...] = lax.dot_general(
+            jnp.where(same, 1.0, 0.0).astype(jnp.bfloat16), jnp.concatenate(chosen, axis=0), (((1,), (1,)), ((), ())),
+            preferred_element_type=jnp.float32,
+        ).astype(jnp.bfloat16)
 
     def arrive(level):
         pair = pl.ds(2 * level, 2)
@@ -336,14 +347,13 @@
                 stage(step, channel)
     await_bytes(from_far, total_sem.at[1])
     base = jnp.sum(recv[1, :, near_devices], axis=1) + from_far[...]
-    early = (KCOH - 3) * 2 * count
     width = halves * BLK
     parts = blocks // halves
     for part in range(parts):
         columns = slice(part * width, (part + 1) * width)
         line = jnp.concatenate([base[part * halves + half : part * halves + half + 1, :] for half in range(halves)], axis=1)
         out_ref[:, columns] = line + jnp.dot(
-            picks[:, :early], staged[:early, columns], preferred_element_type=jnp.float32
+            picks[...], staged[:, columns], preferred_element_type=jnp.float32
         )
     arrive(LEVELS - 1)
     for part in range(parts):
@@ -354,7 +364,7 @@
             high = value.astype(jnp.bfloat16)
             lines += [high, (value - high.astype(jnp.float32)).astype(jnp.bfloat16)]
         out_ref[:, columns] += jnp.dot(
-            picks[:, early:], jnp.concatenate(lines, axis=0), preferred_element_type=jnp.float32
+            last_picks[...], jnp.concatenate(lines, axis=0), preferred_element_type=jnp.float32
         )
 
     for level in range(LEVELS):
@@ -373,6 +383,7 @@
     blocked = lambda array: array.reshape(2, points // BLK, BLK).transpose(1, 0, 2).reshape(2 * points // BLK, BLK)
     hbm = pl.BlockSpec(memory_space=pl.ANY)
     chirps = chirp_table(points, first_rows)
+    factors = twist_factors(points, first_rows)
     block = (2 * points // BLK, BLK)
     summed = pl.pallas_call(
         functools.partial(kernel, count),
@@ -385,6 +396,7 @@
             pltpu.VMEM(block, jnp.float32),
             pltpu.VMEM(block, jnp.float32),
             pltpu.VMEM(chirps.shape, jnp.float32),
+            pltpu.VMEM(factors.shape, jnp.float32),
             pltpu.VMEM((2, second_rows, first_rows), jnp.float32),
             pltpu.VMEM((2 * first_rows, 2 * first_rows), jnp.bfloat16),
             pltpu.VMEM((segments, tracks.shape[0]), jnp.int32),
@@ -400,7 +412,8 @@
             pltpu.VMEM((count // 2, blocks, BLK), jnp.float32),
             pltpu.VMEM((blocks, BLK), jnp.float32),
             pltpu.VMEM((blocks, BLK), jnp.float32),
-            pltpu.VMEM((tracks.shape[0], (KCOH - 1) * 2 * count), jnp.bfloat16),
+            pltpu.VMEM((tracks.shape[0], (KCOH - 3) * 2 * count), jnp.bfloat16),
+            pltpu.VMEM((tracks.shape[0], 4 * count), jnp.bfloat16),
             pltpu.VMEM(((KCOH - 3) * 2 * count, points // count), jnp.bfloat16),
             pltpu.SemaphoreType.DMA((6,)),
             pltpu.SemaphoreType.DMA((LEVELS,)),
@@ -419,7 +432,7 @@
         blocked(strain_series),
         blocked(antenna),
         jnp.asarray(chirps),
-        jnp.asarray(twist_table(points, first_rows)),
+        jnp.asarray(factors),
         jnp.asarray(dft_table(first_rows)),
         tracks.T,
     )

time: 35.9 us -> 35.7 us (level)
  no operation moved by 1% of the time
where the time goes in v9:
time: 35.7 us; the launch traced here: 35.6 us
  Pallas kernels  34.5 us (97%)
  other arithmetic  1.06 us (3%)
    pallas_call x1, Pallas kernels, local(): pl.pallas_call(functools.partial(kernel, count), out_shape=pltpu.VMEM((tr...  34.5 us
    div x1, other arithmetic, local(): return summed / segments  1.06 us

profile of v9, /device:TPU:11, one launch (start us, length us, event | category | flops | bytes accessed | tf_op | source)
XLA Modules:
  0.0 35.6 jit_solution(16884207817679240354)
XLA Ops:
  0.0 34.5 %shard_map.73 = f32[64,4096]{1,0:T(8,128)S(1)} custom-call(s32[1,6]{1,0:T(1,128)} %drift_hbm.1, bf16[1024,128]{1,0:T(8,128)(2,1)} %bitcast.12, f32[1024,128]{1,0:T(8,128)} %bitcast.11, f32[3,2,256,256]{3,2,1,0:T(8,128)} %constant.9.clone.chirp_hbm, f32[2,40,256]{2,1,0:T(8,128)} %constant.10.clone.factors_hbm, bf16[512,512]{1,0:T(8,128)(2,1)} %constant.11.clone.table_hbm, ...), custom_call_target="tpu_custom_call" | custom-call | tf_op jit(solution)/shard_map/pallas_call | solution.py:388
  34.5 1.1 %broadcast_multiply_fusion = f32[64,4096]{1,0:T(8,128)} fusion(f32[64,4096]{1,0:T(8,128)S(1)} %shard_map.73), kind=kLoop, calls=%fused_computation | loop fusion | flops 262144 | bytes 2097152 | tf_op jit(solution)/shard_map/div | solution.py:439

commit v10 on v9

--- a/solution.py
+++ b/solution.py
@@ -16,6 +16,7 @@
 PAD = 8
 HALO = 16
 SUB = 8
+HALVES = DFT_ROWS // BLK
 MESH = pl.DeviceIdType.MESH
 
 chirp_step = 3.0
@@ -46,10 +47,11 @@
 
 
 def kernel(
-    count, drift_hbm, series_hbm, antenna_hbm, chirp_hbm, factors_hbm, table_hbm, tracks_hbm, out_ref,
+    count, drift_hbm, series_hbm, antenna_hbm, chirp_hbm, factors_hbm, table_hbm, tracks_hbm,
+    out_ref, recv, last_picks,
     drift, series_in, series, antenna, chirp, factors, twist, table, tracks,
     strain, weights, weighted, spread, middle, spectra, padded,
-    send, recv, gather, total_far, from_far, picks, last_picks, staged,
+    send, gather, total_far, from_far, picks, staged,
     load_sem, chirp_sem, send_sem, far_sem, near_sem, gather_sem, total_sem, late_sem,
 ):
     _, second_rows, first_rows = strain.shape
@@ -356,23 +358,37 @@
             picks[...], staged[:, columns], preferred_element_type=jnp.float32
         )
     arrive(LEVELS - 1)
-    for part in range(parts):
-        columns = slice(part * width, (part + 1) * width)
-        lines = []
-        for channel in channels[-2:]:
-            value = jnp.concatenate([recv[channel, part * halves + half] for half in range(halves)], axis=1)
-            high = value.astype(jnp.bfloat16)
-            lines += [high, (value - high.astype(jnp.float32)).astype(jnp.bfloat16)]
-        out_ref[:, columns] += jnp.dot(
-            last_picks[...], jnp.concatenate(lines, axis=0), preferred_element_type=jnp.float32
-        )
-
     for level in range(LEVELS):
         pair = pl.ds(2 * level, 2)
         await_bytes(send.at[pair if level else pl.ds(0, 1), pl.ds(0, half_count)], send_sem.at[level])
         await_bytes(send.at[pair, pl.ds(0, half_count - 1)], send_sem.at[LEVELS + level])
     await_bytes(send.at[1, pl.ds(0, half_count - 1)], send_sem.at[2 * LEVELS])
     await_bytes(total_far, total_sem.at[0])
+
+
+def finish(segments, partial_ref, recv_ref, picks_ref, out_hbm, summed, sem):
+    _, blocks, _, lanes = recv_ref.shape
+    parts = blocks // HALVES
+    width = HALVES * lanes
+    group = max(parts // 4, 1)
+    copies = []
+    for part in range(parts):
+        columns = slice(part * width, (part + 1) * width)
+        lines = []
+        for channel in (KCOH - 2, KCOH - 1):
+            value = jnp.concatenate([recv_ref[channel, part * HALVES + half] for half in range(HALVES)], axis=1)
+            high = value.astype(jnp.bfloat16)
+            lines += [high, (value - high.astype(jnp.float32)).astype(jnp.bfloat16)]
+        total = partial_ref[:, columns] + jnp.dot(
+            picks_ref[...], jnp.concatenate(lines, axis=0), preferred_element_type=jnp.float32
+        )
+        summed[:, columns] = total * (1.0 / segments)
+        if (part + 1) % group == 0:
+            done = slice((part + 1 - group) * width, (part + 1) * width)
+            copies.append(pltpu.make_async_copy(summed.at[:, done], out_hbm.at[:, done], sem.at[len(copies)]))
+            copies[-1].start()
+    for copy in copies:
+        copy.wait()
 
 
 def local(count, strain_series, antenna, drift, tracks):
@@ -382,14 +398,19 @@
     blocks = points // count // BLK
     blocked = lambda array: array.reshape(2, points // BLK, BLK).transpose(1, 0, 2).reshape(2 * points // BLK, BLK)
     hbm = pl.BlockSpec(memory_space=pl.ANY)
+    vmem = pl.BlockSpec(memory_space=pltpu.VMEM)
     chirps = chirp_table(points, first_rows)
     factors = twist_factors(points, first_rows)
     block = (2 * points // BLK, BLK)
-    summed = pl.pallas_call(
+    partial, received, picks = pl.pallas_call(
         functools.partial(kernel, count),
-        out_shape=pltpu.VMEM((tracks.shape[0], points // count), jnp.float32),
+        out_shape=(
+            pltpu.VMEM((tracks.shape[0], points // count), jnp.float32),
+            pltpu.VMEM((KCOH, blocks, count, BLK), jnp.float32),
+            pltpu.VMEM((tracks.shape[0], 4 * count), jnp.bfloat16),
+        ),
         in_specs=[hbm] * 7,
-        out_specs=pl.BlockSpec(memory_space=pltpu.VMEM),
+        out_specs=(vmem, vmem, vmem),
         scratch_shapes=[
             pltpu.SMEM(drift.shape, jnp.int32),
             pltpu.VMEM(block, jnp.bfloat16),
@@ -408,12 +429,10 @@
             pltpu.VMEM((4, second_rows + 2 * HALO, first_rows), jnp.float32),
             pltpu.VMEM((2, points // BLK + 2 * PAD, BLK), jnp.float32),
             pltpu.VMEM((KCOH, count, blocks, BLK), jnp.float32),
-            pltpu.VMEM((KCOH, blocks, count, BLK), jnp.float32),
             pltpu.VMEM((count // 2, blocks, BLK), jnp.float32),
             pltpu.VMEM((blocks, BLK), jnp.float32),
             pltpu.VMEM((blocks, BLK), jnp.float32),
             pltpu.VMEM((tracks.shape[0], (KCOH - 3) * 2 * count), jnp.bfloat16),
-            pltpu.VMEM((tracks.shape[0], 4 * count), jnp.bfloat16),
             pltpu.VMEM(((KCOH - 3) * 2 * count, points // count), jnp.bfloat16),
             pltpu.SemaphoreType.DMA((6,)),
             pltpu.SemaphoreType.DMA((LEVELS,)),
@@ -436,7 +455,15 @@
         jnp.asarray(dft_table(first_rows)),
         tracks.T,
     )
-    return summed / segments
+    parts = max(blocks // HALVES, 1)
+    return pl.pallas_call(
+        functools.partial(finish, segments),
+        out_shape=jax.ShapeDtypeStruct(partial.shape, jnp.float32),
+        in_specs=[vmem] * 3,
+        out_specs=hbm,
+        scratch_shapes=[pltpu.VMEM(partial.shape, jnp.float32), pltpu.SemaphoreType.DMA((min(parts, 8),))],
+        compiler_params=pltpu.CompilerParams(vmem_limit_bytes=8 << 20),
+    )(partial, received, picks)
 
 
 def solution(mesh):

time: 35.7 us -> 35.6 us (level)
  other arithmetic: 1.06 us -> 0 us
  Pallas kernels: 34.5 us -> 35.4 us
    div x1 -> x0, other arithmetic: 1.06 us -> none  [local(): return summed / segments]
    pallas_call x1 -> x2, Pallas kernels: 34.5 us -> 35.4 us  [the longest x1 34.2 us: local(): pl.pallas_call(functools.partial(kernel, count), out_shape=(pltpu.VMEM((t...]
where the time goes in v10:
time: 35.6 us; the launch traced here: 35.4 us
  Pallas kernels  35.4 us (99%)
    pallas_call x1, Pallas kernels, local(): pl.pallas_call(functools.partial(kernel, count), out_shape=(pltpu.VMEM((t...  34.2 us
    pallas_call x1, Pallas kernels, local(): pl.pallas_call(functools.partial(finish, segments), out_shape=jax.ShapeDt...  1.21 us

profile of v10, /device:TPU:11, one launch (start us, length us, event | category | flops | bytes accessed | tf_op | source)
XLA Modules:
  0.0 35.4 jit_solution(5577250970400194388)
XLA Ops:
  0.0 34.2 %shard_map.73 = (f32[64,4096]{1,0:T(8,128)S(1)}, f32[6,32,16,128]{3,2,1,0:T(8,128)S(1)}, bf16[64,64]{1,0:T(8,128)(2,1)S(1)}) custom-call(s32[1,6]{1,0:T(1,128)} %drift_hbm.1, bf16[1024,128]{1,0:T(8,128)(2,1)} %bitcast.12, f32[1024,128]{1,0:T(8,128)} %bitcast.11, f32[3,2,256,256]{3,2,1,0:T(8,128)} %constant.6.clone.chirp_hbm, ...), custom_call_target="tpu_custom_call" | custom-call | tf_op jit(solution)/shard_map/pallas_call | solution.py:405
  34.2 1.2 %shard_map.74 = f32[64,4096]{1,0:T(8,128)} custom-call(f32[64,4096]{1,0:T(8,128)S(1)} %get-tuple-element.8.partial_ref, f32[6,32,16,128]{3,2,1,0:T(8,128)S(1)} %get-tuple-element.9.recv_ref, bf16[64,64]{1,0:T(8,128)(2,1)S(1)} %get-tuple-element.10.picks_ref), custom_call_target="tpu_custom_call" | custom-call | tf_op jit(solution)/shard_map/pallas_call | solution.py:459

commit v11 on v10

--- a/solution.py
+++ b/solution.py
@@ -279,28 +279,28 @@
         def _():
             ship_far(0, pl.ds(0, 1), half_count // 2, half_count, ascending=True)
 
-        @pl.when(jnp.logical_and(level == 0, jnp.logical_and(side == 1, is_early)))
-        def _():
-            pl.semaphore_wait(late_sem, late_count)
-
         second_stage(coefs, side * (half_rows + HALO), half_rows - HALO)
         place(level, near, half_count)
 
+        @pl.when(jnp.logical_and(level == 0, jnp.logical_and(side == 1, is_early)))
+        def _():
+            pl.semaphore_wait(late_sem, late_count)
+
         @pl.when(level == 0)
         def _():
             ship_base()
 
-        ship_near(level)
-
-        @pl.when(level > 0)
-        def _():
-            ship_far(level, pl.ds(2 * level, 2))
-
-        @pl.when(level == LEVELS - 2)
+        @pl.when(level == LEVELS - 1)
         def _():
             pltpu.make_async_copy(gather, gather, gather_sem).wait()
             total_far[...] = jnp.sum(gather[...], axis=0)
             push(total_far, from_far, total_sem.at[0], total_sem.at[1], mirror)
+
+        ship_near(level)
+
+        @pl.when(level > 0)
+        def _():
+            ship_far(level, pl.ds(2 * level, 2))
 
         @pl.when(level < LEVELS - 1)
         def _():

time: 35.6 us -> 35.6 us (level)
  no operation moved by 1% of the time
where the time goes in v11:
time: 35.6 us; the launch traced here: 35.4 us
  Pallas kernels  35.4 us (99%)
    pallas_call x1, Pallas kernels, local(): pl.pallas_call(functools.partial(kernel, count), out_shape=(pltpu.VMEM((t...  34.2 us
    pallas_call x1, Pallas kernels, local(): pl.pallas_call(functools.partial(finish, segments), out_shape=jax.ShapeDt...  1.21 us

profile of v11, /device:TPU:11, one launch (start us, length us, event | category | flops | bytes accessed | tf_op | source)
XLA Modules:
  0.0 35.4 jit_solution(6795164710850034711)
XLA Ops:
  0.0 34.2 %shard_map.73 = (f32[64,4096]{1,0:T(8,128)S(1)}, f32[6,32,16,128]{3,2,1,0:T(8,128)S(1)}, bf16[64,64]{1,0:T(8,128)(2,1)S(1)}) custom-call(s32[1,6]{1,0:T(1,128)} %drift_hbm.1, bf16[1024,128]{1,0:T(8,128)(2,1)} %bitcast.12, f32[1024,128]{1,0:T(8,128)} %bitcast.11, f32[3,2,256,256]{3,2,1,0:T(8,128)} %constant.6.clone.chirp_hbm, ...), custom_call_target="tpu_custom_call" | custom-call | tf_op jit(solution)/shard_map/pallas_call | solution.py:405
  34.2 1.2 %shard_map.74 = f32[64,4096]{1,0:T(8,128)} custom-call(f32[64,4096]{1,0:T(8,128)S(1)} %get-tuple-element.8.partial_ref, f32[6,32,16,128]{3,2,1,0:T(8,128)S(1)} %get-tuple-element.9.recv_ref, bf16[64,64]{1,0:T(8,128)(2,1)S(1)} %get-tuple-element.10.picks_ref), custom_call_target="tpu_custom_call" | custom-call | tf_op jit(solution)/shard_map/pallas_call | solution.py:459

commit v12 on v10

--- a/solution.py
+++ b/solution.py
@@ -357,13 +357,14 @@
         out_ref[:, columns] = line + jnp.dot(
             picks[...], staged[:, columns], preferred_element_type=jnp.float32
         )
-    arrive(LEVELS - 1)
     for level in range(LEVELS):
+        if level == LEVELS - 1:
+            await_bytes(send.at[1, pl.ds(0, half_count - 1)], send_sem.at[2 * LEVELS])
+            await_bytes(total_far, total_sem.at[0])
+            arrive(level)
         pair = pl.ds(2 * level, 2)
         await_bytes(send.at[pair if level else pl.ds(0, 1), pl.ds(0, half_count)], send_sem.at[level])
         await_bytes(send.at[pair, pl.ds(0, half_count - 1)], send_sem.at[LEVELS + level])
-    await_bytes(send.at[1, pl.ds(0, half_count - 1)], send_sem.at[2 * LEVELS])
-    await_bytes(total_far, total_sem.at[0])
 
 
 def finish(segments, partial_ref, recv_ref, picks_ref, out_hbm, summed, sem):

time: 35.6 us -> 35.6 us (level)
  no operation moved by 1% of the time
where the time goes in v12:
time: 35.6 us; the launch traced here: 35.4 us
  Pallas kernels  35.4 us (99%)
    pallas_call x1, Pallas kernels, local(): pl.pallas_call(functools.partial(kernel, count), out_shape=(pltpu.VMEM((t...  34.2 us
    pallas_call x1, Pallas kernels, local(): pl.pallas_call(functools.partial(finish, segments), out_shape=jax.ShapeDt...  1.21 us

profile of v12, /device:TPU:11, one launch (start us, length us, event | category | flops | bytes accessed | tf_op | source)
XLA Modules:
  0.0 35.4 jit_solution(2901347777357972282)
XLA Ops:
  0.0 34.2 %shard_map.73 = (f32[64,4096]{1,0:T(8,128)S(1)}, f32[6,32,16,128]{3,2,1,0:T(8,128)S(1)}, bf16[64,64]{1,0:T(8,128)(2,1)S(1)}) custom-call(s32[1,6]{1,0:T(1,128)} %drift_hbm.1, bf16[1024,128]{1,0:T(8,128)(2,1)} %bitcast.12, f32[1024,128]{1,0:T(8,128)} %bitcast.11, f32[3,2,256,256]{3,2,1,0:T(8,128)} %constant.6.clone.chirp_hbm, ...), custom_call_target="tpu_custom_call" | custom-call | tf_op jit(solution)/shard_map/pallas_call | solution.py:406
  34.2 1.2 %shard_map.74 = f32[64,4096]{1,0:T(8,128)} custom-call(f32[64,4096]{1,0:T(8,128)S(1)} %get-tuple-element.8.partial_ref, f32[6,32,16,128]{3,2,1,0:T(8,128)S(1)} %get-tuple-element.9.recv_ref, bf16[64,64]{1,0:T(8,128)(2,1)S(1)} %get-tuple-element.10.picks_ref), custom_call_target="tpu_custom_call" | custom-call | tf_op jit(solution)/shard_map/pallas_call | solution.py:460

commit v13 on v10

--- a/solution.py
+++ b/solution.py
@@ -279,12 +279,12 @@
         def _():
             ship_far(0, pl.ds(0, 1), half_count // 2, half_count, ascending=True)
 
-        @pl.when(jnp.logical_and(level == 0, jnp.logical_and(side == 1, is_early)))
-        def _():
-            pl.semaphore_wait(late_sem, late_count)
-
         second_stage(coefs, side * (half_rows + HALO), half_rows - HALO)
         place(level, near, half_count)
+
+        @pl.when(jnp.logical_and(level == 0, jnp.logical_and(side == 1, is_early)))
+        def _():
+            pl.semaphore_wait(late_sem, late_count)
 
         @pl.when(level == 0)
         def _():

time: 35.6 us -> 35.6 us (level)
  no operation moved by 1% of the time
where the time goes in v13:
time: 35.6 us; the launch traced here: 35.4 us
  Pallas kernels  35.4 us (99%)
    pallas_call x1, Pallas kernels, local(): pl.pallas_call(functools.partial(kernel, count), out_shape=(pltpu.VMEM((t...  34.2 us
    pallas_call x1, Pallas kernels, local(): pl.pallas_call(functools.partial(finish, segments), out_shape=jax.ShapeDt...  1.21 us

profile of v13, /device:TPU:11, one launch (start us, length us, event | category | flops | bytes accessed | tf_op | source)
XLA Modules:
  0.0 35.4 jit_solution(178243965528038787)
XLA Ops:
  0.0 34.2 %shard_map.73 = (f32[64,4096]{1,0:T(8,128)S(1)}, f32[6,32,16,128]{3,2,1,0:T(8,128)S(1)}, bf16[64,64]{1,0:T(8,128)(2,1)S(1)}) custom-call(s32[1,6]{1,0:T(1,128)} %drift_hbm.1, bf16[1024,128]{1,0:T(8,128)(2,1)} %bitcast.12, f32[1024,128]{1,0:T(8,128)} %bitcast.11, f32[3,2,256,256]{3,2,1,0:T(8,128)} %constant.6.clone.chirp_hbm, ...), custom_call_target="tpu_custom_call" | custom-call | tf_op jit(solution)/shard_map/pallas_call | solution.py:405
  34.2 1.2 %shard_map.74 = f32[64,4096]{1,0:T(8,128)} custom-call(f32[64,4096]{1,0:T(8,128)S(1)} %get-tuple-element.8.partial_ref, f32[6,32,16,128]{3,2,1,0:T(8,128)S(1)} %get-tuple-element.9.recv_ref, bf16[64,64]{1,0:T(8,128)(2,1)S(1)} %get-tuple-element.10.picks_ref), custom_call_target="tpu_custom_call" | custom-call | tf_op jit(solution)/shard_map/pallas_call | solution.py:459
